TPU v7x, 256 devices: a whole 4x4x8 slice. The times are simulated.
256 devices in a mesh: node: 64 (over z, x, core), sector: 4 (over y).
Axes of the slice: x: 4, y: 4, z: 8, core: 2. Of those that a mesh axis runs over, the one named last changes fastest.
Arguments:
- returns: bfloat16 [8192, 12, 2048], P('node'), may hold values from -0.29882812 to 0.29882812
- barrier_scale: float32 [8192, 12], P('node'), may hold values from 0.25 to 4
- parent_ids: int32 [8192, 1], P('node'), may hold values from 0 to 63; in each aligned block of 128 rows (0 to 127, 128 to 255, ...) at most 4 rows name the same one
- loadings: float32 [64, 2048], P('node'), may hold values from -3 to 3
- own_variance: float32 [64, 2048], P('node'), may hold values from 0.5 to 4
- sector_sizes: int32 [64], replicated, may hold values from 1 to 64, 2048 in all
Outputs:
- cholesky_rows: float32 [64, 2048, 2048], P('node', 'sector')
Inputs may be any that keep to these rules, and one draw needn't show every extreme that they name: `parent_ids`: of the 128 children held by one index of node (aligned blocks of rows), at most 4 share a parent; in every draw some block has exactly 4 children of one parent. `sector_sizes`: the sizes sum to 2048, and the largest is 64.
All inputs are finite; a program needn't handle non-finite values.
Results may differ from a plain program's by a relative error of at most 0.00045.
Values may be sent and summed in bfloat16 or wider, within the bound.
A program may use at most 192 MiB of HBM per device.

v0:
```python
import jax
import jax.numpy as jnp
from jax import lax
from jax.sharding import PartitionSpec as P


def broadcast(array, axis, root):
    mine = lax.axis_index(axis) == root
    return lax.psum(jnp.where(mine, array, jnp.zeros_like(array)), axis)


def sector_labels(sector_sizes, count):
    sector_ends = jnp.cumsum(sector_sizes)
    asset_index = jnp.arange(count, dtype=jnp.int32)
    return jnp.sum((asset_index[:, None] >= sector_ends[None, :]).astype(jnp.int32), axis=1)


def on_device(returns, barrier_scale, parent_ids, loadings, own_variance, sector_sizes):
    node_count = lax.axis_size("node")
    sector_count = lax.axis_size("sector")
    my_index = lax.axis_index("sector")
    child_count, row_count, asset_count = returns.shape
    capacity = max(2, 2 * child_count // node_count)
    band_rows = asset_count // sector_count
    first_row = my_index * band_rows
    scaled = (jnp.sqrt(barrier_scale)[:, :, None] * returns.astype(jnp.float32)).astype(
        jnp.bfloat16
    )
    targets = parent_ids[:, 0]
    child_index = jnp.arange(child_count, dtype=jnp.int32)
    earlier = (targets[:, None] == targets[None, :]) & (child_index[None, :] < child_index[:, None])
    position = jnp.sum(earlier.astype(jnp.int32), axis=1)
    slot_of = targets * capacity + position
    slot_index = jnp.arange(node_count * capacity, dtype=jnp.int32)
    onehot = (slot_of[None, :] == slot_index[:, None]).astype(jnp.bfloat16)
    flattened = scaled.reshape(child_count, row_count * asset_count)
    outbox = jnp.dot(onehot, flattened, preferred_element_type=jnp.float32).astype(jnp.bfloat16)
    outbox = outbox.reshape(node_count, capacity, row_count, asset_count)
    inbox = lax.all_to_all(outbox, "node", split_axis=0, concat_axis=0, tiled=True)
    rows_all = inbox.reshape(-1, asset_count)
    my_columns = lax.dynamic_slice_in_dim(rows_all, first_row, band_rows, 1)
    schur = lax.dot_general(
        my_columns, rows_all, (((0,), (0,)), ((), ())), preferred_element_type=jnp.float32
    )
    sector_of = sector_labels(sector_sizes, asset_count)
    row_labels = lax.dynamic_slice_in_dim(sector_of, first_row, band_rows)
    loading = loadings[0]
    row_loading = lax.dynamic_slice_in_dim(loading, first_row, band_rows)
    row_variance = lax.dynamic_slice_in_dim(own_variance[0], first_row, band_rows)
    asset_index = jnp.arange(asset_count, dtype=jnp.int32)
    on_diagonal = (
        asset_index[None, :] == (first_row + jnp.arange(band_rows, dtype=jnp.int32))[:, None]
    )
    covariance = jnp.where(
        row_labels[:, None] == sector_of[None, :],
        row_loading[:, None] * loading[None, :],
        jnp.zeros((), jnp.float32),
    )
    normal_matrix = (
        schur
        + covariance
        + jnp.where(on_diagonal, row_variance[:, None], jnp.zeros((), jnp.float32))
    )
    blocks = []
    for step_index in range(sector_count):
        offset = step_index * band_rows
        column_block = normal_matrix[:, offset : offset + band_rows]
        is_root = my_index == step_index
        if offset > 0:
            left_part = jnp.concatenate(blocks, axis=1)
            reduced = column_block - jnp.dot(
                left_part,
                left_part.T,
                precision=lax.Precision.HIGHEST,
                preferred_element_type=jnp.float32,
            )
        else:
            reduced = column_block
        guarded = jnp.where(is_root, reduced, jnp.eye(band_rows, dtype=jnp.float32))
        diag_factor = jnp.linalg.cholesky(guarded)
        if step_index + 1 < sector_count:
            if offset > 0:
                root_panel = jnp.concatenate([left_part, diag_factor], axis=1)
            else:
                root_panel = diag_factor
            arrived_panel = broadcast(root_panel, "sector", step_index)
            root_diag = arrived_panel[:, offset:]
            if offset > 0:
                residual_block = column_block - jnp.dot(
                    left_part,
                    arrived_panel[:, :offset].T,
                    precision=lax.Precision.HIGHEST,
                    preferred_element_type=jnp.float32,
                )
            else:
                residual_block = column_block
            below_diag = jax.scipy.linalg.solve_triangular(
                root_diag, residual_block.T, lower=True
            ).T
            new_block = jnp.where(
                my_index > step_index,
                below_diag,
                jnp.where(is_root, root_diag, jnp.zeros((), jnp.float32)),
            )
        else:
            new_block = jnp.where(is_root, diag_factor, jnp.zeros((), jnp.float32))
        blocks.append(new_block)
    cholesky_rows = jnp.concatenate(blocks, axis=1)
    return cholesky_rows[None]


def solution(mesh):
    in_specs = (
        P("node", None, None),
        P("node", None),
        P("node", None),
        P("node", None),
        P("node", None),
        P(),
    )
    out_specs = P("node", "sector", None)
    return jax.shard_map(
        on_device, mesh=mesh, in_specs=in_specs, out_specs=out_specs, check_vma=False
    )
```

profile of v0, /device:TPU:98, one launch (start us, length us, event | category | flops | bytes accessed | tf_op | source)
XLA Modules:
  0.0 1181.5 jit_solution(5187004120071925878)
XLA Ops:
  6.5 8.7 copy.113
  15.4 4.2 multiply_convert_fusion
  19.6 6.3 convolution_convert_fusion
  25.9 18.6 %reshape.87 = bf16[64,4,12,2048]{3,2,1,0:T(8,128)(2,1)} reshape(bf16[256,24576]{1,0:T(8,128)(2,1)} %convolution_convert_fusion) | data formatting | bytes 25165824 | tf_op jit(solution)/shard_map/reshape | solution.py:38
  44.6 15.9 %copy.114 = bf16[64,4,12,2048]{3,1,2,0:T(4,128)(2,1)} copy(bf16[64,4,12,2048]{3,2,1,0:T(8,128)(2,1)} %reshape.87) | data formatting | bytes 25165824 | tf_op jit(solution)/shard_map/reshape | solution.py:38
  60.4 11.0 all-to-all-start
  73.2 270.7 %all-to-all-done = bf16[64,4,12,2048]{3,1,2,0:T(4,128)(2,1)} async-done(((bf16[64,4,12,2048]{3,1,2,0:T(4,128)(2,1)}), bf16[64,4,12,2048]{3,1,2,0:T(4,128)(2,1)}, u32[]{:S(2)}, u32[]{:S(2)}) %all-to-all-start) | async-done | bytes 12582944 | tf_op jit(solution)/shard_map/all_to_all | solution.py:39
  343.9 14.1 %copy.115 = bf16[64,4,12,2048]{3,2,1,0:T(8,128)(2,1)} copy(bf16[64,4,12,2048]{3,1,2,0:T(4,128)(2,1)} %all-to-all-done) | data formatting | bytes 25165824 | tf_op jit(solution)/shard_map/all_to_all | solution.py:39
  358.0 19.9 %reshape.88 = bf16[3072,2048]{1,0:T(8,128)(2,1)} reshape(bf16[64,4,12,2048]{3,2,1,0:T(8,128)(2,1)} %copy.115) | data formatting | bytes 25165824 | tf_op jit(solution)/shard_map/reshape | solution.py:40
  377.9 11.6 select_add_fusion
  393.1 11.7 cholesky.462
  405.0 9.8 custom-call.34
  417.5 11.7 cholesky.481
  429.3 10.2 custom-call.35
  441.5 11.7 cholesky.502
  453.4 9.8 custom-call.36
  464.8 11.8 %cholesky.519 = f32[128,128]{1,0:T(8,128)S(1)} custom-call(f32[128,128]{1,0:T(8,128)S(1)} %convolution_subtract_fusion.22), custom_call_target="Cholesky" | custom-call | tf_op jit(solution)/shard_map/jit(cholesky)/cholesky | solution.py:80
  483.3 56.2 %all-reduce.5.cloned.1.call-done = f32[512,512]{0,1:T(8,128)} async-done(((f32[512,512]{0,1:T(8,128)}), f32[512,512]{0,1:T(8,128)}) %all-reduce.5.cloned.1.call-update) | async-done | bytes 1048592 | tf_op jit(solution)/shard_map/psum | solution.py:9
  539.5 2.4 fusion.29
  541.9 11.9 %while.6 = (s32[]{:T(128)}, f32[512,512]{0,1:T(8,128)}, s32[4,2]{0,1:T(2,128)S(1)}, f32[4,128,128]{2,1,0:T(8,128)S(1)}, s32[]{:T(128)}) while((s32[]{:T(128)}, f32[512,512]{0,1:T(8,128)}, s32[4,2]{0,1:T(2,128)S(1)}, f32[4,128,128]{2,1,0:T(8,128)S(1)}, s32[]{:T(128)}) %tuple.79), condition=%wide.while_cond, body=%wide.while_body.sunk | while | flops 2 | bytes 393329 | solution.py:97
  542.6 2.2 dynamic-slice.19
  545.6 2.2 dynamic-slice.19
  548.6 2.2 dynamic-slice.19
  551.5 2.2 dynamic-slice.19
  553.8 39.3 %custom-call.37 = f32[4,128,128]{1,2,0:T(8,128)S(1)} custom-call(f32[4,128,128]{2,1,0:T(8,128)S(1)} %get-tuple-element.27), custom_call_target="InvertDiagBlocksLowerTriangular" | custom-call | tf_op jit(solution)/shard_map/jit(_solve_triangular)/triangular_solve | solution.py:97
  599.4 3.1 convert_select_fusion.2
  604.0 11.7 cholesky.534
  615.9 9.8 custom-call.38
  628.8 11.7 cholesky.553
  640.7 9.8 custom-call.39
  652.4 11.7 cholesky.574
  664.2 10.2 custom-call.40
  676.0 11.7 cholesky.591
  694.9 64.9 %all-reduce.7.cloned.1.call-done = f32[512,1024]{0,1:T(8,128)} async-done(((f32[512,1024]{0,1:T(8,128)}), f32[512,1024]{0,1:T(8,128)}) %all-reduce.7.cloned.1.call-update) | async-done | bytes 2097168 | tf_op jit(solution)/shard_map/psum | solution.py:9
  759.7 2.5 fusion.27
  762.2 11.5 while.7
  762.8 2.2 dynamic-slice.21
  765.7 2.2 dynamic-slice.21
  768.6 2.2 dynamic-slice.21
  771.5 2.1 dynamic-slice.21
  774.5 40.3 %custom-call.41 = f32[4,128,128]{1,2,0:T(8,128)S(1)} custom-call(f32[4,128,128]{2,1,0:T(8,128)} %copy-done.9), custom_call_target="InvertDiagBlocksLowerTriangular" | custom-call | tf_op jit(solution)/shard_map/jit(_solve_triangular)/triangular_solve | solution.py:97
  814.8 3.3 fusion.17
  824.2 4.8 convert_select_fusion.1
  832.8 12.1 %cholesky.606 = f32[128,128]{1,0:T(8,128)S(1)} custom-call(f32[128,128]{1,0:T(8,128)S(1)} %cholesky.772), custom_call_target="Cholesky" | custom-call | tf_op jit(solution)/shard_map/jit(cholesky)/cholesky | solution.py:80
  845.0 9.8 custom-call.42
  857.8 11.7 cholesky.625
  869.6 9.8 custom-call.43
  881.3 11.9 %cholesky.646 = f32[128,128]{1,0:T(8,128)S(1)} custom-call(f32[128,128]{1,0:T(8,128)S(1)} %cholesky.781), custom_call_target="Cholesky" | custom-call | tf_op jit(solution)/shard_map/jit(cholesky)/cholesky | solution.py:80
  893.3 9.8 custom-call.44
  904.8 11.7 cholesky.663
  924.1 80.8 %all-reduce.9.cloned.1.call-done = f32[512,1536]{0,1:T(8,128)} async-done(((f32[512,1536]{0,1:T(8,128)}), f32[512,1536]{0,1:T(8,128)}) %all-reduce.9.cloned.1.call-update) | async-done | bytes 3145744 | tf_op jit(solution)/shard_map/psum | solution.py:9
  1006.2 8.0 while.8
  1014.9 40.5 %custom-call.45 = f32[4,128,128]{1,2,0:T(8,128)S(1)} custom-call(f32[4,128,128]{2,1,0:T(8,128)} %copy-done.10), custom_call_target="InvertDiagBlocksLowerTriangular" | custom-call | tf_op jit(solution)/shard_map/jit(_solve_triangular)/triangular_solve | solution.py:97
  1055.5 5.4 fusion.14
  1066.6 6.5 convert_select_fusion
  1077.0 11.7 cholesky.678
  1088.9 9.8 custom-call.46
  1101.6 11.7 cholesky.697
  1113.4 10.0 custom-call.47
  1125.3 11.7 cholesky.718
  1137.1 9.8 custom-call.48
  1148.6 11.7 cholesky.735
  1165.8 3.6 maximum_bitcast_fusion
  1169.4 5.3 copy.149
  (245 shorter events, 92.5 us)
Async XLA Ops:
  6.5 8.7 copy-start.11
  6.5 8.7 copy-start.14
  60.4 11.6 copy-start.12
  60.4 12.1 %copy-start.13 = (f32[1,2048]{1,0:T(1,128)S(1)}, f32[1,2048]{1,0:T(1,128)}, u32[]{:S(2)}) copy-start(f32[1,2048]{1,0:T(1,128)} %param.12) | copy-start | bytes 24580
  60.4 283.5 %all-to-all-start = ((bf16[64,4,12,2048]{3,1,2,0:T(4,128)(2,1)}), bf16[64,4,12,2048]{3,1,2,0:T(4,128)(2,1)}, u32[]{:S(2)}, u32[]{:S(2)}) async-start(bf16[64,4,12,2048]{3,1,2,0:T(4,128)(2,1)} %copy.114), calls=%async_computation | async-start | bytes 25165824 | tf_op jit(solution)/shard_map/all_to_all | solution.py:39
  71.5 468.1 %all-reduce.5.cloned.1.call-start = ((), (), s32[]{:S(2)}) async-start(), calls=%async_computation.1 | async-start | bytes 2097152 | tf_op jit(solution)/shard_map/psum | solution.py:9
  389.6 2.0 copy-start.3
  392.1 1.0 copy-start.6
  483.2 276.5 %all-reduce.7.cloned.1.call-start = ((), (), s32[]{:S(2)}) async-start(), calls=%async_computation.2 | async-start | bytes 4194304 | tf_op jit(solution)/shard_map/psum | solution.py:9
  541.9 57.2 %copy-start.2 = (f32[512,512]{0,1:T(8,128)S(1)}, f32[512,512]{0,1:T(8,128)}, u32[]{:S(2)}) copy-start(f32[512,512]{0,1:T(8,128)} %all-reduce.5.cloned.1.call-done) | copy-start | bytes 3145732
  603.0 1.0 copy-start.7
  694.8 310.1 %all-reduce.9.cloned.1.call-start = ((), (), s32[]{:S(2)}) async-start(), calls=%async_computation.3 | async-start | bytes 6291456 | tf_op jit(solution)/shard_map/psum | solution.py:9
  759.7 55.1 %copy-start = (f32[512,1024]{0,1:T(8,128)S(1)}, f32[512,1024]{0,1:T(8,128)}, u32[]{:S(2)}) copy-start(f32[512,1024]{0,1:T(8,128)} %all-reduce.7.cloned.1.call-done) | copy-start | bytes 6291460
  773.7 0.7 copy-start.9
  814.8 9.2 copy-start.1
  831.8 1.0 copy-start.8
  1014.2 0.7 copy-start.10
  1065.7 1.0 copy-start.4
  1076.0 1.0 copy-start.5
Sparse Core Ops, SparseCore 0:
  483.4 56.1 all-reduce.4
  694.9 64.7 all-reduce.6
  924.2 80.6 all-reduce.8
where the time goes:
time: 1190 us; the launch traced here: 1180 us
  waiting for transfers between devices  473 us (40%)
  other arithmetic  463 us (39%)
  local copies, waits for them, and re-layouts  128 us (11%)
  matrix products  80.6 us (7%)
  between operations  24.6 us (2%)
    another operation x60, other arithmetic, on_device(): diag_factor = jnp.linalg.cholesky(guarded)  318 us
    all_to_all x1, waiting for transfers between devices, on_device(): lax.all_to_all(outbox, 'node', split_axis=0, concat_axis=0, tiled=True)  271 us
    psum x3, waiting for transfers between devices, broadcast(): return lax.psum(jnp.where(mine, array, jnp.zeros_like(array)), axis)  202 us
    another operation x7, other arithmetic, on_device(): jax.scipy.linalg.solve_triangular(root_diag, residual_block.T, lower=True)  126 us
    reshape x2, local copies, waits for them, and re-layouts, on_device(): outbox = outbox.reshape(node_count, capacity, row_count, asset_count)  34.5 us
    another operation x64, local copies, waits for them, and re-layouts, on_device(): jax.scipy.linalg.solve_triangular(root_diag, residual_block.T, lower=True)  31 us
    another operation x24, matrix products, on_device(): diag_factor = jnp.linalg.cholesky(guarded)  24.7 us
  transfers between devices with their start and end apart: 4, of which 4 were waited for; matrix products, arithmetic and copies ran while one was open for 0% of the time, Pallas kernels for 0%

commit v1 on v0

v1 whole, which is shorter than its diff:
```python
import functools

import jax
import jax.numpy as jnp
from jax import lax
from jax.experimental import pallas as pl
from jax.experimental.pallas import tpu as pltpu
from jax.sharding import PartitionSpec as P

F32 = jnp.float32
BF = jnp.bfloat16

def sub(x,k): return jnp.broadcast_to(x[k:k+1,:],(8,128))
def lane(x,k): return jnp.broadcast_to(x[:,k:k+1],(8,128))

def chol128(load, u_ref, inv_ref):
    row=lax.broadcasted_iota(jnp.int32,(8,128),0); col=lax.broadcasted_iota(jnp.int32,(8,128),1)
    wa=[load(g) for g in range(16)]
    wi=[jnp.where(col==row+8*g,1.0,0.0).astype(F32) for g in range(16)]
    for g in range(16):
        p,pi=wa[g],wi[g]
        nxt=g<15
        if nxt: r,ri=wa[g+1],wi[g+1]
        c=[lane(p,8*g+m) for m in range(8)]
        if nxt: cr=[lane(r,8*g+m) for m in range(8)]
        dvec=jnp.ones((8,128),F32)
        for k in range(8):
            dk=sub(c[k],k)
            inv=1.0/dk
            mk=jnp.where(row>k,c[k]*inv,0.0)
            prow,pirow=sub(p,k),sub(pi,k)
            if nxt: mr=cr[k]*inv
            for m in range(k+1,8):
                dkm=sub(c[m],k)
                c[m]=c[m]-mk*dkm
                if nxt: cr[m]=cr[m]-mr*dkm
            p=p-mk*prow; pi=pi-mk*pirow
            if nxt:
                r=r-mr*prow; ri=ri-mr*pirow
            dvec=jnp.where(row==k,dk,dvec)
        rs=lax.rsqrt(dvec)
        q=jnp.where(col>=row+8*g,p*rs,0.0); qi=pi*rs
        u_ref[8*g:8*g+8,:]=q; inv_ref[8*g:8*g+8,:]=qi
        if nxt: wa[g+1],wi[g+1]=r,ri
        if g<14:
            t=q.T
            qr=[sub(q,k) for k in range(8)]; qir=[sub(qi,k) for k in range(8)]
            for G in range(g+2,16):
                tg=t[8*G:8*G+8,:]
                a,b=wa[G],wi[G]
                for k in range(8):
                    tk=jnp.broadcast_to(tg[:,k:k+1],(8,128))
                    a=a-tk*qr[k]; b=b-tk*qir[k]
                wa[G],wi[G]=a,b


NT=(((1,),(1,)),((),()))
NN=(((1,),(0,)),((),()))
def dot(a,b,dims): return lax.dot_general(a,b,dims,preferred_element_type=F32)
def split(x):
    h=x.astype(BF); return h,(x-h.astype(F32)).astype(BF)
def dot3(a,b,dims):
    ah,al=split(a); bh,bl=split(b)
    return dot(ah,bh,dims)+(dot(al,bh,dims)+dot(ah,bl,dims))

def kern(mode, n, rows, s_ref, r_ref, lrow, lcol, frow, fcol, vrow, o_ref, a, rt, xl, xr, u0, i0, u1, i1, inv):
    nt=n//256
    ir=lax.broadcasted_iota(jnp.int32,(256,256),0); ic=lax.broadcasted_iota(jnp.int32,(256,256),1)
    eye=jnp.where(ir==ic,1.0,0.0)
    eyeb=eye.astype(BF)
    def al(x,m): return pl.multiple_of(x,m)
    def strip(i): return r_ref.at[i//2, :, pl.ds(al((i%2)*256,256),256)]
    if "S" in mode:
        def srow(i,_):
            src=strip(i)
            for kk in range(rows//512):
                rt[:,kk*512:(kk+1)*512]=dot(eyeb,src[kk*512:(kk+1)*512,:],NT).astype(BF)
            ri=pl.ds(al(i*256,256),256)
            lc=jnp.broadcast_to(lcol[ri,0:1],(256,256)); fc=jnp.broadcast_to(fcol[ri,0:1],(256,256))
            def scol(k,_):
                ki=pl.ds(al(k*256,256),256)
                s=dot(rt[...],strip(k)[...],NN)
                s=s+jnp.where(lc==lrow[:,ki],fc*frow[:,ki],0.0)
                s=s+jnp.where((ir==ic)&(i==k),vrow[:,ki],0.0)
                a[ri,ki]=s
                return 0
            lax.fori_loop(0,i+1,scol,0)
            return 0
        lax.fori_loop(0,nt,srow,0)
    if "C" in mode:
        def panel(p,_):
            c0=al(p*256,256); c1=al(p*256+128,128)
            chol128(lambda g:a[pl.ds(al(c0+8*g,8),8),pl.ds(c0,128)], u0, i0)
            x10=dot3(a[pl.ds(c1,128),pl.ds(c0,128)],i0[...],NT)
            a[pl.ds(c1,128),pl.ds(c0,128)]=x10
            a[pl.ds(c1,128),pl.ds(c1,128)]=a[pl.ds(c1,128),pl.ds(c1,128)]-dot3(x10,x10,NT)
            a[pl.ds(c0,128),pl.ds(c0,128)]=u0[...].T
            chol128(lambda g:a[pl.ds(al(c1+8*g,8),8),pl.ds(c1,128)], u1, i1)
            a[pl.ds(c1,128),pl.ds(c1,128)]=u1[...].T
            m=-dot3(i1[...],dot3(x10,i0[...],NN),NN)
            def put(rs,cs,v):
                h,l=split(v)
                inv[rs:rs+128,cs:cs+128]=h; inv[rs:rs+128,256+cs:256+cs+128]=h; inv[rs:rs+128,512+cs:512+cs+128]=l
            z=jnp.zeros((128,128),F32)
            put(0,0,i0[...]); put(0,128,z); put(128,0,m); put(128,128,i1[...])
            def trsm(t,_):
                ti=pl.ds(al(t*256,256),256)
                h,l=split(a[ti,pl.ds(c0,256)])
                x=dot(jnp.concatenate([h,l,h],axis=1),inv[...],NT)
                a[ti,pl.ds(c0,256)]=x
                h,l=split(x)
                xl[ti,0:256]=h; xl[ti,256:512]=l; xl[ti,512:768]=h
                xr[ti,0:256]=h; xr[ti,256:512]=h; xr[ti,512:768]=l
                return 0
            lax.fori_loop(p+1,nt,trsm,0)
            def trail(t,_):
                ti=pl.ds(al(t*256,256),256)
                def inner(k,_):
                    ki=pl.ds(al(k*256,256),256)
                    a[ti,ki]=a[ti,ki]-dot(xl[ti,:],xr[ki,:],NT)
                    return 0
                lax.fori_loop(p+1,t+1,inner,0)
                return 0
            lax.fori_loop(p+1,nt,trail,0)
            return 0
        lax.fori_loop(0,nt,panel,0)
    s=s_ref[0]
    def outp(b,_):
        r0=al(s*512+b*64,64)
        rr=lax.broadcasted_iota(jnp.int32,(64,n),0)+r0; cc=lax.broadcasted_iota(jnp.int32,(64,n),1)
        o_ref[pl.ds(al(b*64,64),64),:]=jnp.where(cc<=rr,a[pl.ds(r0,64),:],0.0)
        return 0
    lax.fori_loop(0,8,outp,0)

def factor(sidx, r, labels, loading, variance, mode="SC"):
    n=labels.shape[0]; rows=r.shape[1]
    V=pl.BlockSpec(memory_space=pltpu.VMEM)
    return pl.pallas_call(functools.partial(kern,mode,n,rows),
        out_shape=jax.ShapeDtypeStruct((512,n),F32),
        in_specs=[pl.BlockSpec(memory_space=pltpu.SMEM)]+[V]*6, out_specs=V,
        scratch_shapes=[pltpu.VMEM((n,n),F32),pltpu.VMEM((256,rows),BF),pltpu.VMEM((n,768),BF),pltpu.VMEM((n,768),BF)]
          +[pltpu.VMEM((128,128),F32)]*4+[pltpu.VMEM((256,768),BF)],
        compiler_params=pltpu.CompilerParams(vmem_limit_bytes=62*1024*1024),
    )(sidx, r, labels[None,:], labels[:,None], loading[None,:], loading[:,None], variance[None,:])


def gather_kernel(capacity, idx_ref, x_ref, o_ref):
    rows = x_ref.shape[1]

    def target(t, _):
        pieces = []
        for c in range(capacity):
            child = idx_ref[t * capacity + c]
            block = x_ref[jnp.maximum(child, 0)].astype(F32)
            pieces.append(jnp.where(child >= 0, block, 0.0))
        height = capacity * rows
        o_ref[pl.ds(pl.multiple_of(t * height, 16), height), :] = jnp.concatenate(pieces, axis=0).astype(BF)
        return 0

    lax.fori_loop(0, idx_ref.shape[0] // capacity, target, 0)


def gather_rows(idx, x, capacity):
    return pl.pallas_call(
        functools.partial(gather_kernel, capacity),
        out_shape=jax.ShapeDtypeStruct((idx.shape[0] * x.shape[1], x.shape[2]), BF),
        in_specs=[pl.BlockSpec(memory_space=pltpu.SMEM), pl.BlockSpec(memory_space=pltpu.VMEM)],
        out_specs=pl.BlockSpec(memory_space=pltpu.VMEM),
    )(idx, x)


def sector_labels(sector_sizes, count):
    sector_ends = jnp.cumsum(sector_sizes)
    asset_index = jnp.arange(count, dtype=jnp.int32)
    return jnp.sum((asset_index[:, None] >= sector_ends[None, :]).astype(jnp.int32), axis=1)


def on_device(returns, barrier_scale, parent_ids, loadings, own_variance, sector_sizes):
    node_count = lax.axis_size("node")
    sector_count = lax.axis_size("sector")
    my_index = lax.axis_index("sector")
    child_count, row_count, asset_count = returns.shape
    capacity = 4
    band = asset_count // sector_count
    mine = lax.dynamic_slice_in_dim(returns, my_index * band, band, 2)
    scaled = (jnp.sqrt(barrier_scale)[:, :, None] * mine.astype(F32)).astype(BF)
    targets = parent_ids[:, 0]
    child_index = jnp.arange(child_count, dtype=jnp.int32)
    earlier = (targets[:, None] == targets[None, :]) & (child_index[None, :] < child_index[:, None])
    position = jnp.sum(earlier.astype(jnp.int32), axis=1)
    slot_of = targets * capacity + position
    slots = jnp.arange(node_count * capacity, dtype=jnp.int32)
    idx = jnp.max(jnp.where(slot_of[None, :] == slots[:, None], child_index[None, :], -1), axis=1)
    outbox = gather_rows(idx, scaled, capacity)
    inbox = lax.all_to_all(outbox, "node", split_axis=0, concat_axis=0, tiled=True)
    quarters = lax.all_gather(inbox, "sector", axis=0, tiled=False)
    labels = sector_labels(sector_sizes, asset_count)
    out = factor(my_index[None].astype(jnp.int32), quarters, labels, loadings[0], own_variance[0])
    return out[None]


def solution(mesh):
    in_specs = (
        P("node", None, None),
        P("node", None),
        P("node", None),
        P("node", None),
        P("node", None),
        P(),
    )
    return jax.shard_map(
        on_device, mesh=mesh, in_specs=in_specs, out_specs=P("node", "sector", None), check_vma=False
    )
```

time: 1190 us -> 382 us (0.32)
  other arithmetic: 463 us -> 4.95 us
  waiting for transfers between devices: 473 us -> 116 us
  Pallas kernels: 0 us -> 157 us
  local copies, waits for them, and re-layouts: 128 us -> 5.81 us
  blocking collectives: 0 us -> 83 us
  matrix products: 80.6 us -> 0 us
    another operation x69 -> x2, other arithmetic: 445 us -> 0.2 us  [the longest x60 318 us: on_device(): diag_factor = jnp.linalg.cholesky(guarded)]
    all_to_all x1 -> x0, waiting for transfers between devices: 271 us -> none  [on_device(): lax.all_to_all(outbox, 'node', split_axis=0, concat_axis=0, tiled=True)]
    psum x3 -> x0, waiting for transfers between devices: 202 us -> none  [broadcast(): return lax.psum(jnp.where(mine, array, jnp.zeros_like(array)), axis)]
    pallas_call x0 -> x2, Pallas kernels: none -> 157 us  [the longest x1 152 us: factor(): pl.pallas_call(functools.partial(kern, mode, n, rows), out_shape=jax.Shap...]
    all_gather x0 -> x1, waiting for transfers between devices: none -> 116 us  [on_device(): quarters = lax.all_gather(inbox, 'sector', axis=0, tiled=False)]
    all_to_all x0 -> x1, blocking collectives: none -> 83 us  [on_device(): lax.all_to_all(outbox, 'node', split_axis=0, concat_axis=0, tiled=True)]
    reshape x3 -> x0, local copies, waits for them, and re-layouts: 54.4 us -> none  [the longest x2 34.5 us: on_device(): outbox = outbox.reshape(node_count, capacity, row_count, asset_count)]
    dot_general x7 -> x0, matrix products: 40.9 us -> none  [the longest x3 14.3 us: on_device(): jnp.dot(left_part, left_part.T, precision=lax.Precision.HIGHEST, preferre...]
  transfers between devices with their start and end apart: 4 -> 1, of which waited for: 4 -> 1; matrix products, arithmetic and copies ran while one was open for 0% -> 1% of each run, Pallas kernels for 0% -> 0%
where the time goes in v1:
time: 382 us; the launch traced here: 380 us
  Pallas kernels  157 us (41%)
  waiting for transfers between devices  116 us (30%)
  blocking collectives  83 us (22%)
  between operations  13.4 us (4%)
  local copies, waits for them, and re-layouts  5.81 us (2%)
  other arithmetic  4.95 us (1%)
    pallas_call x1, Pallas kernels, factor(): pl.pallas_call(functools.partial(kern, mode, n, rows), out_shape=jax.Shap...  152 us
    all_gather x1, waiting for transfers between devices, on_device(): quarters = lax.all_gather(inbox, 'sector', axis=0, tiled=False)  116 us
    all_to_all x1, blocking collectives, on_device(): lax.all_to_all(outbox, 'node', split_axis=0, concat_axis=0, tiled=True)  83 us
  transfers between devices with their start and end apart: 1, of which 1 were waited for; matrix products, arithmetic and copies ran while one was open for 1% of the time, Pallas kernels for 0%

profile of v1, /device:TPU:98, one launch (start us, length us, event | category | flops | bytes accessed | tf_op | source)
XLA Modules:
  0.0 379.7 jit_solution(8406782148960221288)
XLA Ops:
  6.5 0.0 all-gather.2.cloned.1.call-start
  6.5 0.9 convert_reduce_fusion.1
  7.4 0.7 multiply_add_fusion
  8.1 0.7 select_reduce_fusion.idx_ref
  8.8 0.7 sqrt.3
  9.5 0.1 copy.20
  9.6 1.5 constant_dynamic-slice_fusion
  11.2 2.3 multiply_convert_fusion.x_ref
  13.5 4.9 %shard_map.64 = bf16[3072,512]{1,0:T(8,128)(2,1)} custom-call(s32[256]{0:T(256)} %select_reduce_fusion.idx_ref, bf16[128,12,512]{2,1,0:T(8,128)(2,1)} %multiply_convert_fusion.x_ref), custom_call_target="tpu_custom_call" | custom-call | tf_op jit(solution)/shard_map/pallas_call | solution.py:164
  18.4 83.0 %all_to_all.9 = bf16[64,48,512]{2,1,0:T(8,128)(2,1)} all-to-all(bf16[64,48,512]{2,1,0:T(8,128)(2,1)} %bitcast.11), channel_id=1, replica_groups=mesh['node'=64,'sector'=4] {'node'}, dimensions={0} | all-to-all | bytes 6291456 | tf_op jit(solution)/shard_map/all_to_all | solution.py:195
  101.3 0.0 copy-start.2
  101.3 0.0 copy-start.1
  101.3 0.0 all-gather.2.cloned.1.call-update
  101.4 0.6 copy-done.2
  102.0 0.1 copy.22
  102.1 0.1 reduce-window.8
  102.2 0.1 reduce
  102.3 0.1 convert_reduce_fusion
  102.5 0.0 copy-start
  102.5 1.4 copy.23.lcol
  103.8 0.0 copy-done.1
  103.8 1.4 copy.24.fcol
  105.2 115.8 %all-gather.2.cloned.1.call-done.r_ref = bf16[4,3072,512]{2,1,0:T(8,128)(2,1)} async-done(((bf16[1,3072,512]{2,1,0:T(8,128)(2,1)}), bf16[4,3072,512]{2,1,0:T(8,128)(2,1)}) %all-gather.2.cloned.1.call-update) | async-done | bytes 12582928 | tf_op jit(solution)/shard_map/all_gather | solution.py:196
  221.0 0.0 copy-done
  221.0 151.8 %shard_map.65 = f32[512,2048]{1,0:T(8,128)} custom-call(s32[1]{0:T(128)} %bitcast.s_ref, bf16[4,3072,512]{2,1,0:T(8,128)(2,1)} %all-gather.2.cloned.1.call-done.r_ref, s32[1,2048]{1,0:T(1,128)} %bitcast.13, s32[2048,1]{1,0:T(8,128)} %copy.23.lcol, f32[1,2048]{1,0:T(1,128)} %frow.1, f32[2048,1]{1,0:T(8,128)} %copy.24.fcol, f32[1,2048]{1,0:T(1,128)} %vrow.1), custom_call_target="tpu_custom_call" | custom-call | tf_op jit(solution)/shard_map/pallas_call | solution.py:138
Async XLA Ops:
  6.5 214.5 %all-gather.2.cloned.1.call-start = ((), (), s32[]{:S(2)}) async-start(), calls=%async_computation.1 | async-start | bytes 15728640 | tf_op jit(solution)/shard_map/all_gather | solution.py:196
  101.3 0.7 copy-start.2
  101.3 2.5 copy-start.1
  102.5 118.6 %copy-start = (s32[2048]{0:T(1024)}, s32[2048]{0:T(1024)S(1)}, u32[]{:S(2)}) copy-start(s32[2048]{0:T(1024)S(1)} %convert_reduce_fusion) | copy-start | bytes 24580
Sparse Core Ops, SparseCore 0:
  101.5 119.4 all-gather.1

commit v2 on v1

--- a/solution.py
+++ b/solution.py
@@ -69,7 +69,7 @@
     eye=jnp.where(ir==ic,1.0,0.0)
     eyeb=eye.astype(BF)
     def al(x,m): return pl.multiple_of(x,m)
-    def strip(i): return r_ref.at[i//2, :, pl.ds(al((i%2)*256,256),256)]
+    def strip(i): return r_ref.at[i]
     if "S" in mode:
         def srow(i,_):
             src=strip(i)
@@ -144,29 +144,145 @@
     )(sidx, r, labels[None,:], labels[:,None], loading[None,:], loading[:,None], variance[None,:])
 
 
-def gather_kernel(capacity, idx_ref, x_ref, o_ref):
-    rows = x_ref.shape[1]
-
-    def target(t, _):
-        pieces = []
-        for c in range(capacity):
-            child = idx_ref[t * capacity + c]
-            block = x_ref[jnp.maximum(child, 0)].astype(F32)
-            pieces.append(jnp.where(child >= 0, block, 0.0))
-        height = capacity * rows
-        o_ref[pl.ds(pl.multiple_of(t * height, 16), height), :] = jnp.concatenate(pieces, axis=0).astype(BF)
-        return 0
-
-    lax.fori_loop(0, idx_ref.shape[0] // capacity, target, 0)
-
-
-def gather_rows(idx, x, capacity):
+MESH = pl.DeviceIdType.MESH
+ORDER = (0, 1, 7, 2, 6, 3, 5, 4)
+
+
+def prep_kernel(s_ref, targets_ref, scale_ref, x_ref, o_ref):
+    rows, children, width = x_ref.shape
+    targets = targets_ref[...]
+    across = jnp.broadcast_to(targets.astype(F32), (children, children))
+    first = lax.broadcasted_iota(jnp.int32, (children, children), 0)
+    second = lax.broadcasted_iota(jnp.int32, (children, children), 1)
+    earlier = (across.T == across) & (first < second)
+    position = jnp.sum(jnp.where(earlier, 1.0, 0.0), axis=0, keepdims=True).astype(jnp.int32)
+    slot = targets * 4 + position
+    scale = jnp.concatenate([scale_ref[...], jnp.zeros((16 - rows, children), F32)], axis=0).T
+    count = o_ref.shape[1]
+    out_row = lax.broadcasted_iota(jnp.int32, (count * 16, children), 0)
+    row_slot = (out_row // 16) * 4 + out_row % 4
+    hit = row_slot == jnp.broadcast_to(slot, (count * 16, children))
+    lane_of = (out_row // 4) % 4
+    picks = jnp.concatenate(
+        [jnp.where(hit & (lane_of == k), 1.0, 0.0).astype(BF) for k in range(4)], axis=1
+    )
+    for quad in range(rows // 4):
+        scaled = []
+        for k in range(4):
+            r = quad * 4 + k
+            scaled.append((scale[:, r : r + 1] * x_ref[r].astype(F32)).astype(BF))
+        moved = dot(picks, jnp.concatenate(scaled, axis=0), NN).astype(BF)
+        for h in range(2):
+            half = moved[:, h * 256 : (h + 1) * 256]
+            o_ref[h, :, quad * 16 : (quad + 1) * 16, :] = half.reshape(count, 16, 256)
+
+
+def prepare(sector, targets, scale, planes):
+    rows, children, assets = planes.shape
+    width = 512
     return pl.pallas_call(
-        functools.partial(gather_kernel, capacity),
-        out_shape=jax.ShapeDtypeStruct((idx.shape[0] * x.shape[1], x.shape[2]), BF),
-        in_specs=[pl.BlockSpec(memory_space=pltpu.SMEM), pl.BlockSpec(memory_space=pltpu.VMEM)],
-        out_specs=pl.BlockSpec(memory_space=pltpu.VMEM),
-    )(idx, x)
+        prep_kernel,
+        out_shape=jax.ShapeDtypeStruct((2, 64, rows * 4, 256), BF),
+        grid_spec=pltpu.PrefetchScalarGridSpec(
+            num_scalar_prefetch=1,
+            grid=(1,),
+            in_specs=[
+                pl.BlockSpec((1, children), lambda i, s: (0, 0)),
+                pl.BlockSpec((rows, children), lambda i, s: (0, 0)),
+                pl.BlockSpec((rows, children, width), lambda i, s: (0, 0, s[0])),
+            ],
+            out_specs=pl.BlockSpec((2, 64, rows * 4, 256), lambda i, s: (0, 0, 0, 0)),
+        ),
+    )(sector, targets, scale, planes)
+
+
+def exchange_kernel(out_ref, r_ref, ls, ss, rs, ys, yr, zs, zr):
+    n = lax.axis_index("node")
+    s = lax.axis_index("sector")
+    z, w = n // 8, n % 8
+    up, down = (s + 1) % 4, (s + 3) % 4
+
+    def plane(h, j, i):
+        t = ((z + 8 - j) % 8) * 8 + (w + 8 - i) % 8
+        return pltpu.make_async_remote_copy(
+            out_ref.at[h, t], r_ref.at[2 * s + h, n], ss.at[h], rs.at[h, j],
+            device_id=(t, s), device_id_type=MESH)
+
+    def group(strip, j, there, send, recv):
+        rows = pl.ds(((z + j) % 8) * 8, 8)
+        return pltpu.make_async_remote_copy(
+            r_ref.at[strip, rows], r_ref.at[strip, rows], send, recv,
+            device_id=(n, there), device_id_type=MESH)
+
+    def own(h, j, d):
+        return group(2 * s + h, j, (up, down)[d], ys.at[d, h], yr.at[d, h, j])
+
+    def arriving(h, j, d):
+        return group(2 * ((down, up)[d]) + h, j, (up, down)[d], ys.at[d, h], yr.at[d, h, j])
+
+    def relay(j, d):
+        return group(2 * ((down, up)[d]) + d, j, (up, down)[d], zs.at[d], zr.at[d, j])
+
+    def relayed(j, d):
+        return group(2 * ((s + 2) % 4) + d, j, (up, down)[d], zs.at[d], zr.at[d, j])
+
+    mine = [pltpu.make_async_copy(out_ref.at[h, n], r_ref.at[2 * s + h, n], ls.at[h]) for h in range(2)]
+    for c in mine:
+        c.start()
+    for j in ORDER:
+        def send(i, _, j=j):
+            plane(0, j, i).start()
+            plane(1, j, i).start()
+            return 0
+        lax.fori_loop(1 if j == 0 else 0, 8, send, 0)
+    last = None
+    for j in ORDER + (None,):
+        if j is not None:
+            for h in range(2):
+                count = 7 if j == 0 else 8
+                blocks = r_ref.at[2 * s + h, pl.ds(((z + j) % 8) * 8, count)]
+                pltpu.make_async_remote_copy(
+                    blocks, blocks, ss.at[h], rs.at[h, j], device_id=(n, up), device_id_type=MESH
+                ).wait_recv()
+                if j == 0:
+                    mine[h].wait()
+            for h in range(2):
+                for d in range(2):
+                    own(h, j, d).start()
+        if last is not None:
+            for d in range(2):
+                arriving(d, last, d).wait_recv()
+                relay(last, d).start()
+        last = j
+    for j in ORDER:
+        for d in range(2):
+            arriving(1 - d, j, d).wait_recv()
+            relayed(j, d).wait_recv()
+    for h in range(2):
+        blocks = out_ref.at[h, pl.ds(0, 63)]
+        pltpu.make_async_remote_copy(
+            blocks, blocks, ss.at[h], rs.at[h, 0], device_id=(n, up), device_id_type=MESH
+        ).wait_send()
+    for d in range(2):
+        for h in range(2):
+            pltpu.make_async_remote_copy(
+                r_ref.at[0], r_ref.at[0], ys.at[d, h], yr.at[d, h, 0], device_id=(n, up), device_id_type=MESH
+            ).wait_send()
+        pltpu.make_async_remote_copy(
+            r_ref.at[0], r_ref.at[0], zs.at[d], zr.at[d, 0], device_id=(n, up), device_id_type=MESH
+        ).wait_send()
+
+
+def exchange(outbox):
+    dma = pltpu.SemaphoreType.DMA
+    return pl.pallas_call(
+        exchange_kernel,
+        out_shape=jax.ShapeDtypeStruct((8,) + outbox.shape[1:], BF),
+        in_specs=[pl.BlockSpec(memory_space=pl.ANY)],
+        out_specs=pl.BlockSpec(memory_space=pl.ANY),
+        scratch_shapes=[dma((2,)), dma((2,)), dma((2, 8)), dma((2, 2)), dma((2, 2, 8)), dma((2,)), dma((2, 8))],
+        compiler_params=pltpu.CompilerParams(has_side_effects=True),
+    )(outbox)
 
 
 def sector_labels(sector_sizes, count):
@@ -176,26 +292,18 @@
 
 
 def on_device(returns, barrier_scale, parent_ids, loadings, own_variance, sector_sizes):
-    node_count = lax.axis_size("node")
-    sector_count = lax.axis_size("sector")
-    my_index = lax.axis_index("sector")
     child_count, row_count, asset_count = returns.shape
-    capacity = 4
-    band = asset_count // sector_count
-    mine = lax.dynamic_slice_in_dim(returns, my_index * band, band, 2)
-    scaled = (jnp.sqrt(barrier_scale)[:, :, None] * mine.astype(F32)).astype(BF)
-    targets = parent_ids[:, 0]
-    child_index = jnp.arange(child_count, dtype=jnp.int32)
-    earlier = (targets[:, None] == targets[None, :]) & (child_index[None, :] < child_index[:, None])
-    position = jnp.sum(earlier.astype(jnp.int32), axis=1)
-    slot_of = targets * capacity + position
-    slots = jnp.arange(node_count * capacity, dtype=jnp.int32)
-    idx = jnp.max(jnp.where(slot_of[None, :] == slots[:, None], child_index[None, :], -1), axis=1)
-    outbox = gather_rows(idx, scaled, capacity)
-    inbox = lax.all_to_all(outbox, "node", split_axis=0, concat_axis=0, tiled=True)
-    quarters = lax.all_gather(inbox, "sector", axis=0, tiled=False)
+    sector = lax.axis_index("sector")[None].astype(jnp.int32)
+    outbox = prepare(
+        sector,
+        parent_ids.reshape(1, child_count),
+        jnp.sqrt(barrier_scale).T,
+        returns.transpose(1, 0, 2),
+    )
+    strips = exchange(outbox)
+    strips = strips.reshape(8, -1, 256)
     labels = sector_labels(sector_sizes, asset_count)
-    out = factor(my_index[None].astype(jnp.int32), quarters, labels, loadings[0], own_variance[0])
+    out = factor(sector, strips, labels, loadings[0], own_variance[0])
     return out[None]
 
 

time: 382 us -> 304 us (0.80)
  the two profiles are of different devices: /device:TPU:98 before, /device:TPU:134 now
where the time goes in v2:
time: 304 us
  Pallas kernels  298 us (98%)
  local copies, waits for them, and re-layouts  5.51 us (2%)
    pallas_call x1, Pallas kernels, factor(): pl.pallas_call(functools.partial(kern, mode, n, rows), out_shape=jax.Shap...  151 us
    pallas_call x1, Pallas kernels, exchange(): pl.pallas_call(exchange_kernel, out_shape=jax.ShapeDtypeStruct((8,) + out...  141 us

profile of v2, /device:TPU:134, one launch (start us, length us, event | category | flops | bytes accessed | tf_op | source)
XLA Modules:
  0.0 303.5 jit_solution(17667937314419132246)
XLA Ops:
  0.0 1.3 sqrt_bitcast_fusion.scale_ref
  1.3 0.7 copy.11
  2.0 0.1 reduce-window.8
  2.1 0.1 reduce
  2.2 0.1 convert_reduce_fusion
  2.4 0.0 copy-start
  2.4 1.4 copy.12.lcol
  3.8 2.0 copy.13.fcol
  5.9 5.2 %shard_map.64.out_ref = bf16[2,64,48,256]{3,2,1,0:T(8,128)(2,1)} custom-call(s32[1]{0:T(128)} %bitcast.s_ref, s32[1,128]{1,0:T(1,128)} %bitcast.17, f32[12,128]{1,0:T(8,128)} %sqrt_bitcast_fusion.scale_ref, bf16[12,128,2048]{2,1,0:T(8,128)(2,1)} %bitcast.12), custom_call_target="tpu_custom_call" | custom-call | tf_op jit(solution)/shard_map/pallas_call | solution.py:183
  11.0 141.0 %shard_map.65 = bf16[8,64,48,256]{3,2,1,0:T(8,128)(2,1)} custom-call(bf16[2,64,48,256]{3,2,1,0:T(8,128)(2,1)} %shard_map.64.out_ref), custom_call_target="tpu_custom_call" | custom-call | tf_op jit(solution)/shard_map/pallas_call | solution.py:278
  152.0 0.0 copy-done
  152.0 151.5 %shard_map.66 = f32[512,2048]{1,0:T(8,128)} custom-call(s32[1]{0:T(128)} %bitcast.s_ref, bf16[8,3072,256]{2,1,0:T(8,128)(2,1)} %bitcast.11, s32[1,2048]{1,0:T(1,128)} %bitcast.14, s32[2048,1]{1,0:T(8,128)} %copy.12.lcol, f32[1,2048]{1,0:T(1,128)} %frow.1, f32[2048,1]{1,0:T(8,128)} %copy.13.fcol, f32[1,2048]{1,0:T(1,128)} %vrow.1), custom_call_target="tpu_custom_call" | custom-call | tf_op jit(solution)/shard_map/pallas_call | solution.py:138
Async XLA Ops:
  2.4 149.6 %copy-start = (s32[2048]{0:T(1024)}, s32[2048]{0:T(1024)S(1)}, u32[]{:S(2)}) copy-start(s32[2048]{0:T(1024)S(1)} %convert_reduce_fusion) | copy-start | bytes 24580

commit v3 on v2

v3 whole, which is shorter than its diff:
```python
import functools
import types

import jax
import jax.numpy as jnp
from jax import lax
from jax.experimental import pallas as pl
from jax.experimental.pallas import tpu as pltpu
from jax.sharding import PartitionSpec as P

F32 = jnp.float32
BF = jnp.bfloat16


def sub(x,k): return jnp.broadcast_to(x[k:k+1,:],(8,128))
def lane(x,k): return jnp.broadcast_to(x[:,k:k+1],(8,128))

def chol128(load, u_ref, inv_ref):
    row=lax.broadcasted_iota(jnp.int32,(8,128),0); col=lax.broadcasted_iota(jnp.int32,(8,128),1)
    wa=[load(g) for g in range(16)]
    wi=[jnp.where(col==row+8*g,1.0,0.0).astype(F32) for g in range(16)]
    for g in range(16):
        p,pi=wa[g],wi[g]
        nxt=g<15
        if nxt: r,ri=wa[g+1],wi[g+1]
        c=[lane(p,8*g+m) for m in range(8)]
        if nxt: cr=[lane(r,8*g+m) for m in range(8)]
        dvec=jnp.ones((8,128),F32)
        for k in range(8):
            dk=sub(c[k],k)
            inv=1.0/dk
            mk=jnp.where(row>k,c[k]*inv,0.0)
            prow,pirow=sub(p,k),sub(pi,k)
            if nxt: mr=cr[k]*inv
            for m in range(k+1,8):
                dkm=sub(c[m],k)
                c[m]=c[m]-mk*dkm
                if nxt: cr[m]=cr[m]-mr*dkm
            p=p-mk*prow; pi=pi-mk*pirow
            if nxt:
                r=r-mr*prow; ri=ri-mr*pirow
            dvec=jnp.where(row==k,dk,dvec)
        rs=lax.rsqrt(dvec)
        q=jnp.where(col>=row+8*g,p*rs,0.0); qi=pi*rs
        u_ref[8*g:8*g+8,:]=q; inv_ref[8*g:8*g+8,:]=qi
        if nxt: wa[g+1],wi[g+1]=r,ri
        if g<14:
            t=q.T
            qr=[sub(q,k) for k in range(8)]; qir=[sub(qi,k) for k in range(8)]
            for G in range(g+2,16):
                tg=t[8*G:8*G+8,:]
                a,b=wa[G],wi[G]
                for k in range(8):
                    tk=jnp.broadcast_to(tg[:,k:k+1],(8,128))
                    a=a-tk*qr[k]; b=b-tk*qir[k]
                wa[G],wi[G]=a,b


NT = (((1,), (1,)), ((), ()))
NN = (((1,), (0,)), ((), ()))


def dot(a, b, dims):
    return lax.dot_general(a, b, dims, preferred_element_type=F32)


def split(x):
    high = x.astype(BF)
    return high, (x - high.astype(F32)).astype(BF)


def dot3(a, b, dims):
    ah, al = split(a)
    bh, bl = split(b)
    return dot(ah, bh, dims) + (dot(al, bh, dims) + dot(ah, bl, dims))


def tile(i, size=256):
    return pl.ds(pl.multiple_of(i * size, size), size)


def span(start, size, m=128):
    return pl.ds(pl.multiple_of(start, m), size)


def make_normal(c, lo, hi):
    ir = lax.broadcasted_iota(jnp.int32, (256, 256), 0)
    ic = lax.broadcasted_iota(jnp.int32, (256, 256), 1)
    eye = jnp.where(ir == ic, 1.0, 0.0).astype(BF)
    depth = c.r.shape[1]

    def strip(i, _):
        for part in range(depth // 512):
            rows = slice(part * 512, (part + 1) * 512)
            c.rt[:, rows] = dot(eye, c.r[i, rows, :], NT).astype(BF)
        ri = tile(i)
        labels = jnp.broadcast_to(c.lcol[ri, 0:1], (256, 256))
        loading = jnp.broadcast_to(c.fcol[ri, 0:1], (256, 256))

        def block(k, _):
            ki = tile(k)
            total = dot(c.rt[...], c.r[k], NN)
            total = total + jnp.where(labels == c.lrow[:, ki], loading * c.frow[:, ki], 0.0)
            total = total + jnp.where((ir == ic) & (i == k), c.vrow[:, ki], 0.0)
            c.a[ri, ki] = total
            return 0

        lax.fori_loop(0, i + 1, block, 0)
        return 0

    lax.fori_loop(lo, hi, strip, 0)


def diagonal(c, p, event):
    c0, c1 = span(p * 256, 128), span(p * 256 + 128, 128)
    event(2 * p)
    chol128(lambda g: c.a[span(p * 256 + 8 * g, 8, 8), c0], c.u, c.i0)
    c.a[c0, c0] = c.u[...].T
    below = dot3(c.a[c1, c0], c.i0[...], NT)
    c.a[c1, c0] = below
    c.a[c1, c1] = c.a[c1, c1] - dot3(below, below, NT)
    event(2 * p + 1)
    chol128(lambda g: c.a[span(p * 256 + 128 + 8 * g, 8, 8), c1], c.u, c.i1)
    c.a[c1, c1] = c.u[...].T
    corner = -dot3(c.i1[...], dot3(below, c.i0[...], NN), NN)
    zero = jnp.zeros((128, 128), F32)
    for rs, cs, v in ((0, 0, c.i0[...]), (0, 128, zero), (128, 0, corner), (128, 128, c.i1[...])):
        high, low = split(v)
        for at, part in ((0, high), (256, high), (512, low)):
            c.inv[p, rs : rs + 128, at + cs : at + cs + 128] = part


def solve(c, p, lo, hi):
    def one(t, _):
        ti, pi = tile(t), tile(p)
        high, low = split(c.a[ti, pi])
        x = dot(jnp.concatenate([high, low, high], axis=1), c.inv[p], NT)
        c.a[ti, pi] = x
        high, low = split(x)
        c.lh[ti, pi] = high
        c.ll[ti, pi] = low
        return 0

    lax.fori_loop(lo, hi, one, 0)


def update(c, p, lo, hi):
    def one(t, _):
        ti, pi = tile(t), tile(p)

        def block(k, _):
            ki = tile(k)
            high, low = c.lh[ti, pi], c.ll[ti, pi]
            other, other_low = c.lh[ki, pi], c.ll[ki, pi]
            c.a[ti, ki] = c.a[ti, ki] - dot(
                jnp.concatenate([high, low, high], axis=1),
                jnp.concatenate([other, other, other_low], axis=1), NT)
            return 0

        lax.fori_loop(p + 1, t + 1, block, 0)
        return 0

    lax.fori_loop(lo, hi, one, 0)


def write_band(c, s):
    n = c.a.shape[1]

    def rows(b, _):
        r0 = s * 512 + b * 64
        rr = lax.broadcasted_iota(jnp.int32, (64, n), 0) + r0
        cc = lax.broadcasted_iota(jnp.int32, (64, n), 1)
        c.o[tile(b, 64), :] = jnp.where(cc <= rr, c.a[span(r0, 64, 64), :], 0.0)
        return 0

    lax.fori_loop(0, 8, rows, 0)


def factor_scratch(n, rows):
    return dict(
        a=pltpu.VMEM((n, n), F32), rt=pltpu.VMEM((256, rows), BF),
        lh=pltpu.VMEM((n, n), BF), ll=pltpu.VMEM((n, n), BF),
        u=pltpu.VMEM((128, 128), F32), i0=pltpu.VMEM((128, 128), F32), i1=pltpu.VMEM((128, 128), F32),
        inv=pltpu.VMEM((n // 256, 256, 768), BF),
    )


def factor_steps(c, event, second):
    make_normal(c, 0, 4)

    def panel(p, _):
        hi = 4 + 4 * (p // 4)
        diagonal(c, p, event)
        solve(c, p, p + 1, hi)
        update(c, p, p + 1, hi)

        @pl.when(p == 3)
        def _():
            second()
            make_normal(c, 4, 8)

            def again(q, _):
                solve(c, q, 4, 8)
                update(c, q, 4, 8)
                return 0

            lax.fori_loop(0, 4, again, 0)

        return 0

    lax.fori_loop(0, 8, panel, 0)


MESH = pl.DeviceIdType.MESH


def prep_kernel(s_ref, targets_ref, scale_ref, x0_ref, x1_ref, o_ref):
    rows, children, width = x0_ref.shape
    targets = targets_ref[...]
    across = jnp.broadcast_to(targets.astype(F32), (children, children))
    first = lax.broadcasted_iota(jnp.int32, (children, children), 0)
    second = lax.broadcasted_iota(jnp.int32, (children, children), 1)
    earlier = (across.T == across) & (first < second)
    position = jnp.sum(jnp.where(earlier, 1.0, 0.0), axis=0, keepdims=True).astype(jnp.int32)
    slot = targets * 4 + position
    scale = jnp.concatenate([scale_ref[...], jnp.zeros((16 - rows, children), F32)], axis=0).T
    count = o_ref.shape[1]
    out_row = lax.broadcasted_iota(jnp.int32, (count * 16, children), 0)
    row_slot = (out_row // 16) * 4 + out_row % 4
    hit = row_slot == jnp.broadcast_to(slot, (count * 16, children))
    lane_of = (out_row // 4) % 4
    picks = jnp.concatenate(
        [jnp.where(hit & (lane_of == k), 1.0, 0.0).astype(BF) for k in range(4)], axis=1
    )
    for quad in range(rows // 4):
        for h, x_ref in enumerate((x0_ref, x1_ref)):
            scaled = []
            for k in range(4):
                r = quad * 4 + k
                scaled.append((scale[:, r : r + 1] * x_ref[r].astype(F32)).astype(BF))
            moved = dot(picks, jnp.concatenate(scaled, axis=0), NN).astype(BF)
            o_ref[h, :, quad * 16 : (quad + 1) * 16, :] = moved.reshape(count, 16, width)


def prepare(sector, targets, scale, planes):
    rows, children, assets = planes.shape
    width = 256
    return pl.pallas_call(
        prep_kernel,
        out_shape=jax.ShapeDtypeStruct((2, 64, rows * 4, 256), BF),
        grid_spec=pltpu.PrefetchScalarGridSpec(
            num_scalar_prefetch=1,
            grid=(1,),
            in_specs=[
                pl.BlockSpec((1, children), lambda i, s: (0, 0)),
                pl.BlockSpec((rows, children), lambda i, s: (0, 0)),
                pl.BlockSpec((rows, children, width), lambda i, s: (0, 0, s[0])),
                pl.BlockSpec((rows, children, width), lambda i, s: (0, 0, s[0] + 4)),
            ],
            out_specs=pl.BlockSpec((2, 64, rows * 4, 256), lambda i, s: (0, 0, 0, 0)),
        ),
    )(sector, targets, scale, planes, planes)


def sequence(q):
    return ((q % 2) * ((q + 1) // 2) + (1 - q % 2) * (8 - q // 2)) % 8


NAMES = ("a", "rt", "lh", "ll", "u", "i0", "i1", "inv")


def main_kernel(out_ref, lrow, lcol, frow, fcol, vrow, o_ref, r, ls, ss, rs, ys, yr, zs, zr, *scratch):
    n = lax.axis_index("node")
    s = lax.axis_index("sector")
    z, w = n // 8, n % 8
    up, down = (s + 1) % 4, (s + 3) % 4
    there = (up, down)
    c = types.SimpleNamespace(
        r=r, lrow=lrow, lcol=lcol, frow=frow, fcol=fcol, vrow=vrow, o=o_ref, **dict(zip(NAMES, scratch)))

    def send(h, q, i):
        t = ((z + 8 - sequence(q)) % 8) * 8 + (w + 8 - i) % 8
        pltpu.make_async_remote_copy(
            out_ref.at[h, t], r.at[4 * h + s, tile(n, 48)], ss.at[h], rs.at[h, q],
            device_id=(t, s), device_id_type=MESH).start()

    def landed(h, q, count):
        rows = r.at[4 * h + s, span(((z + sequence(q)) % 8) * 384, 48 * count, 48)]
        pltpu.make_async_remote_copy(
            rows, rows, ss.at[h], rs.at[h, q], device_id=(n, up), device_id_type=MESH).wait_recv()

    def group(strip, q, d, sent, got):
        rows = r.at[strip, tile((z + sequence(q)) % 8, 384)]
        return pltpu.make_async_remote_copy(
            rows, rows, sent, got, device_id=(n, there[d]), device_id_type=MESH)

    def own(h, q, d):
        return group(4 * h + s, q, d, ys.at[h, d], yr.at[h, d, q])

    def arriving(h, q, d):
        return group(4 * h + there[1 - d], q, d, ys.at[h, d], yr.at[h, d, q])

    def relay(h, q, d):
        return group(4 * h + there[1 - d], q, d, zs.at[h, d], zr.at[h, q])

    def relayed(h, q):
        return group(4 * h + (s + 2) % 4, q, 0, zs.at[h, 0], zr.at[h, q])

    def forward(h, q):
        for d in range(2):
            own(h, q, d).start()

    def pass_on(h, q, d):
        arriving(h, q, d).wait_recv()
        relay(h, q, d).start()

    def finish(h):
        def one(q, _):
            arriving(h, 2 * q, 1).wait_recv()
            arriving(h, 2 * q + 1, 0).wait_recv()
            relayed(h, 2 * q).wait_recv()
            relayed(h, 2 * q + 1).wait_recv()
            return 0

        lax.fori_loop(0, 4, one, 0)

    mine = [
        pltpu.make_async_copy(out_ref.at[h, n], r.at[4 * h + s, tile(n, 48)], ls.at[h]) for h in range(2)
    ]
    for m in mine:
        m.start()
    for h in range(2):
        def near(i, _, h=h):
            send(h, 0, i)
            return 0

        def far(q, _, h=h):
            def one(i, _):
                send(h, q, i)
                return 0

            lax.fori_loop(0, 8, one, 0)
            return 0

        lax.fori_loop(1, 8, near, 0)
        lax.fori_loop(1, 8, far, 0)

    landed(0, 0, 7)
    mine[0].wait()
    forward(0, 0)
    landed(0, 1, 8)
    forward(0, 1)

    def step(e, _):
        for b in range(2):
            landed(0, 2 * e + b, 8)
            forward(0, 2 * e + b)
            pass_on(0, 2 * e - 2 + b, b)
        return 0

    lax.fori_loop(1, 4, step, 0)
    pass_on(0, 6, 0)
    pass_on(0, 7, 1)
    finish(0)

    def event(e):
        @pl.when(e == 0)
        def _():
            landed(1, 0, 7)
            mine[1].wait()
            forward(1, 0)
            landed(1, 1, 8)
            forward(1, 1)

        @pl.when((e > 0) & (e < 4))
        def _():
            for b in range(2):
                landed(1, 2 * e + b, 8)
                forward(1, 2 * e + b)

        @pl.when((e > 0) & (e < 5))
        def _():
            for b in range(2):
                pass_on(1, 2 * e - 2 + b, b)

    factor_steps(c, event, lambda: finish(1))
    write_band(c, s)

    for h in range(2):
        blocks = out_ref.at[h, pl.ds(0, 63)]
        pltpu.make_async_remote_copy(
            blocks, blocks, ss.at[h], rs.at[h, 0], device_id=(n, up), device_id_type=MESH
        ).wait_send()
        for d in range(2):
            pltpu.make_async_remote_copy(
                r.at[0], r.at[0], ys.at[h, d], yr.at[h, d, 0], device_id=(n, up), device_id_type=MESH
            ).wait_send()
            half = r.at[0, pl.ds(0, 1536)]
            pltpu.make_async_remote_copy(
                half, half, zs.at[h, d], zr.at[h, 0], device_id=(n, up), device_id_type=MESH
            ).wait_send()


def exchange_and_factor(outbox, labels, loading, variance):
    dma = pltpu.SemaphoreType.DMA
    n = labels.shape[0]
    rows = outbox.shape[1] * outbox.shape[2]
    vmem = pl.BlockSpec(memory_space=pltpu.VMEM)
    scratch = factor_scratch(n, rows)
    return pl.pallas_call(
        main_kernel,
        out_shape=jax.ShapeDtypeStruct((n // 4, n), F32),
        in_specs=[pl.BlockSpec(memory_space=pl.ANY)] + [vmem] * 5,
        out_specs=vmem,
        scratch_shapes=[pltpu.VMEM((8, rows, 256), BF), dma((2,)), dma((2,)), dma((2, 8)), dma((2, 2)),
                        dma((2, 2, 8)), dma((2, 2)), dma((2, 8))] + [scratch[k] for k in NAMES],
        compiler_params=pltpu.CompilerParams(has_side_effects=True, vmem_limit_bytes=63 * 1024 * 1024),
    )(outbox, labels[None, :], labels[:, None], loading[None, :], loading[:, None], variance[None, :])


def sector_labels(sector_sizes, count):
    sector_ends = jnp.cumsum(sector_sizes)
    asset_index = jnp.arange(count, dtype=jnp.int32)
    return jnp.sum((asset_index[:, None] >= sector_ends[None, :]).astype(jnp.int32), axis=1)


def on_device(returns, barrier_scale, parent_ids, loadings, own_variance, sector_sizes):
    child_count, row_count, asset_count = returns.shape
    sector = lax.axis_index("sector")[None].astype(jnp.int32)
    outbox = prepare(
        sector,
        parent_ids.reshape(1, child_count),
        jnp.sqrt(barrier_scale).T,
        returns.transpose(1, 0, 2),
    )
    labels = sector_labels(sector_sizes, asset_count)
    out = exchange_and_factor(outbox, labels, loadings[0], own_variance[0])
    return out[None]


def solution(mesh):
    in_specs = (
        P("node", None, None),
        P("node", None),
        P("node", None),
        P("node", None),
        P("node", None),
        P(),
    )
    return jax.shard_map(
        on_device, mesh=mesh, in_specs=in_specs, out_specs=P("node", "sector", None), check_vma=False
    )
```

time: 304 us -> 264 us (0.87)
  the two profiles are of different devices: /device:TPU:134 before, /device:TPU:98 now
where the time goes in v3:
time: 264 us
  Pallas kernels  253 us (96%)
  local copies, waits for them, and re-layouts  10.2 us (4%)
    pallas_call x1, Pallas kernels, exchange_and_factor(): pl.pallas_call(main_kernel, out_shape=jax.ShapeDtypeStruct((n // 4, n), F...  248 us

profile of v3, /device:TPU:98, one launch (start us, length us, event | category | flops | bytes accessed | tf_op | source)
XLA Modules:
  0.0 263.9 jit_solution(10482212325329084864)
XLA Ops:
  0.0 1.3 sqrt_bitcast_fusion.scale_ref
  1.3 0.7 copy.11
  2.0 0.1 reduce-window.8
  2.1 0.1 reduce
  2.2 0.1 convert_reduce_fusion
  2.4 0.0 copy-start
  2.4 1.4 copy.12.lcol
  3.8 2.1 copy.13.fcol
  5.8 5.1 %shard_map.64.out_ref = bf16[2,64,48,256]{3,2,1,0:T(8,128)(2,1)} custom-call(s32[1]{0:T(128)} %bitcast.s_ref, s32[1,128]{1,0:T(1,128)} %bitcast.16, f32[12,128]{1,0:T(8,128)} %sqrt_bitcast_fusion.scale_ref, bf16[12,128,2048]{2,1,0:T(8,128)(2,1)} %bitcast.10, bf16[12,128,2048]{2,1,0:T(8,128)(2,1)} %bitcast.11), custom_call_target="tpu_custom_call" | custom-call | tf_op jit(solution)/shard_map/pallas_call | solution.py:248
  11.0 0.0 copy-done
  11.0 248.2 %shard_map.65 = f32[512,2048]{1,0:T(8,128)} custom-call(bf16[2,64,48,256]{3,2,1,0:T(8,128)(2,1)} %shard_map.64.out_ref, s32[1,2048]{1,0:T(1,128)} %bitcast.14, s32[2048,1]{1,0:T(8,128)} %copy.12.lcol, f32[1,2048]{1,0:T(1,128)} %frow.1, f32[2048,1]{1,0:T(8,128)} %copy.13.fcol, f32[1,2048]{1,0:T(1,128)} %vrow.1), custom_call_target="tpu_custom_call" | custom-call | tf_op jit(solution)/shard_map/pallas_call | solution.py:410
  259.2 4.7 %copy.15 = f32[1,512,2048]{2,1,0:T(8,128)} copy(f32[1,512,2048]{2,1,0:T(8,128)} %bitcast.12) | data formatting | bytes 8388608
Async XLA Ops:
  2.4 8.6 %copy-start = (s32[2048]{0:T(1024)}, s32[2048]{0:T(1024)S(1)}, u32[]{:S(2)}) copy-start(s32[2048]{0:T(1024)S(1)} %convert_reduce_fusion) | copy-start | bytes 24580

commit v4 on v3

--- a/solution.py
+++ b/solution.py
@@ -12,48 +12,77 @@
 BF = jnp.bfloat16
 
 
-def sub(x,k): return jnp.broadcast_to(x[k:k+1,:],(8,128))
-def lane(x,k): return jnp.broadcast_to(x[:,k:k+1],(8,128))
+def sub(x, k):
+    return jnp.broadcast_to(x[k : k + 1, :], (8, 128))
+
+
+def lane(x, k):
+    return jnp.broadcast_to(x[:, k : k + 1], (8, 128))
+
+
+def eliminate(p, pi, near, g, row):
+    c = [lane(p, 8 * g + m) for m in range(8)]
+    cs = [[lane(a, 8 * g + m) for m in range(8)] for a, _ in near]
+    near = [list(x) for x in near]
+    pivots = jnp.ones((8, 128), F32)
+    for k in range(0, 8, 2):
+        a, b, d = sub(c[k], k), sub(c[k + 1], k), sub(c[k + 1], k + 1)
+        det = a * d - b * b
+        ia = 1.0 / a
+        id1 = a * (1.0 / det)
+        ratio = b * ia
+        m0 = jnp.where(row > k, c[k] * ia, 0.0)
+        m1 = jnp.where(row > k + 1, (c[k + 1] - c[k] * ratio) * id1, 0.0)
+        p0, pi0 = sub(p, k), sub(pi, k)
+        p1, pi1 = sub(p, k + 1) - ratio * p0, sub(pi, k + 1) - ratio * pi0
+        es = {}
+        for m in range(k + 2, 8):
+            e0 = sub(c[m], k)
+            es[m] = (e0, sub(c[m], k + 1) - ratio * e0)
+            c[m] = c[m] - m0 * es[m][0] - m1 * es[m][1]
+        p = p - m0 * p0 - m1 * p1
+        pi = pi - m0 * pi0 - m1 * pi1
+        for x, cr in zip(near, cs):
+            n0 = cr[k] * ia
+            n1 = (cr[k + 1] - cr[k] * ratio) * id1
+            for m in range(k + 2, 8):
+                cr[m] = cr[m] - n0 * es[m][0] - n1 * es[m][1]
+            x[0] = x[0] - n0 * p0 - n1 * p1
+            x[1] = x[1] - n0 * pi0 - n1 * pi1
+        pivots = jnp.where(row == k, a, jnp.where(row == k + 1, det * ia, pivots))
+    scale = lax.rsqrt(pivots)
+    return p * scale, pi * scale, near
+
 
 def chol128(load, u_ref, inv_ref):
-    row=lax.broadcasted_iota(jnp.int32,(8,128),0); col=lax.broadcasted_iota(jnp.int32,(8,128),1)
-    wa=[load(g) for g in range(16)]
-    wi=[jnp.where(col==row+8*g,1.0,0.0).astype(F32) for g in range(16)]
-    for g in range(16):
-        p,pi=wa[g],wi[g]
-        nxt=g<15
-        if nxt: r,ri=wa[g+1],wi[g+1]
-        c=[lane(p,8*g+m) for m in range(8)]
-        if nxt: cr=[lane(r,8*g+m) for m in range(8)]
-        dvec=jnp.ones((8,128),F32)
-        for k in range(8):
-            dk=sub(c[k],k)
-            inv=1.0/dk
-            mk=jnp.where(row>k,c[k]*inv,0.0)
-            prow,pirow=sub(p,k),sub(pi,k)
-            if nxt: mr=cr[k]*inv
-            for m in range(k+1,8):
-                dkm=sub(c[m],k)
-                c[m]=c[m]-mk*dkm
-                if nxt: cr[m]=cr[m]-mr*dkm
-            p=p-mk*prow; pi=pi-mk*pirow
-            if nxt:
-                r=r-mr*prow; ri=ri-mr*pirow
-            dvec=jnp.where(row==k,dk,dvec)
-        rs=lax.rsqrt(dvec)
-        q=jnp.where(col>=row+8*g,p*rs,0.0); qi=pi*rs
-        u_ref[8*g:8*g+8,:]=q; inv_ref[8*g:8*g+8,:]=qi
-        if nxt: wa[g+1],wi[g+1]=r,ri
-        if g<14:
-            t=q.T
-            qr=[sub(q,k) for k in range(8)]; qir=[sub(qi,k) for k in range(8)]
-            for G in range(g+2,16):
-                tg=t[8*G:8*G+8,:]
-                a,b=wa[G],wi[G]
-                for k in range(8):
-                    tk=jnp.broadcast_to(tg[:,k:k+1],(8,128))
-                    a=a-tk*qr[k]; b=b-tk*qir[k]
-                wa[G],wi[G]=a,b
+    row = lax.broadcasted_iota(jnp.int32, (8, 128), 0)
+    col = lax.broadcasted_iota(jnp.int32, (8, 128), 1)
+    n = 4
+    wa = [load(g) for g in range(16)]
+    wi = [jnp.where(col == row + 8 * g, 1.0, 0.0).astype(F32) for g in range(16)]
+    for start in range(0, 16, n):
+        qs, qis = [], []
+        for g in range(start, start + n):
+            near = [(wa[x], wi[x]) for x in range(g + 1, start + n)]
+            q, qi, near = eliminate(wa[g], wi[g], near, g, row)
+            for x, (a, b) in zip(range(g + 1, start + n), near):
+                wa[x], wi[x] = a, b
+            q = jnp.where(col >= row + 8 * g, q, 0.0)
+            u_ref[8 * g : 8 * g + 8, :] = q
+            inv_ref[8 * g : 8 * g + 8, :] = qi
+            qs.append(q)
+            qis.append(qi)
+        if start + n < 16:
+            q = jnp.concatenate(qs, axis=0)
+            full = jnp.concatenate([q, jnp.concatenate(qis, axis=0)], axis=1)
+            qh = full.astype(BF)
+            ql = (full - qh.astype(F32)).astype(BF)
+            left = jnp.concatenate([qh[:, :128], ql[:, :128], qh[:, :128]], axis=0)
+            right = jnp.concatenate([qh, qh, ql], axis=0)
+            moved = lax.dot_general(left, right, (((0,), (0,)), ((), ())), preferred_element_type=F32)
+            for x in range(start + n, 16):
+                wa[x] = wa[x] - moved[8 * x : 8 * x + 8, :128]
+                wi[x] = wi[x] - moved[8 * x : 8 * x + 8, 128:]
 
 
 NT = (((1,), (1,)), ((), ()))
@@ -81,6 +110,10 @@
 
 def span(start, size, m=128):
     return pl.ds(pl.multiple_of(start, m), size)
+
+
+def column(row_ref, cols):
+    return jnp.broadcast_to(row_ref[:, cols], (256, 256)).T
 
 
 def make_normal(c, lo, hi):
@@ -94,8 +127,8 @@
             rows = slice(part * 512, (part + 1) * 512)
             c.rt[:, rows] = dot(eye, c.r[i, rows, :], NT).astype(BF)
         ri = tile(i)
-        labels = jnp.broadcast_to(c.lcol[ri, 0:1], (256, 256))
-        loading = jnp.broadcast_to(c.fcol[ri, 0:1], (256, 256))
+        labels = column(c.lrow, ri)
+        loading = column(c.frow, ri)
 
         def block(k, _):
             ki = tile(k)
@@ -111,23 +144,110 @@
     lax.fori_loop(lo, hi, strip, 0)
 
 
-def diagonal(c, p, event):
+def start_normal(c, hi):
+    ir = lax.broadcasted_iota(jnp.int32, (256, 256), 0)
+    ic = lax.broadcasted_iota(jnp.int32, (256, 256), 1)
+
+    def strip(i, _):
+        ri = tile(i)
+        labels = column(c.lrow, ri)
+        loading = column(c.frow, ri)
+
+        def block(k, _):
+            ki = tile(k)
+            total = jnp.where(labels == c.lrow[:, ki], loading * c.frow[:, ki], 0.0)
+            c.a[ri, ki] = total + jnp.where((ir == ic) & (i == k), c.vrow[:, ki], 0.0)
+            return 0
+
+        lax.fori_loop(0, i + 1, block, 0)
+        return 0
+
+    lax.fori_loop(0, hi, strip, 0)
+
+
+def add_rows(c, start, hi):
+    ir = lax.broadcasted_iota(jnp.int32, (256, 256), 0)
+    ic = lax.broadcasted_iota(jnp.int32, (256, 256), 1)
+    eye = jnp.where(ir == ic, 1.0, 0.0).astype(BF)
+    rows = span(start, 384)
+
+    def strip(i, _):
+        turned = dot(eye, c.r[i, rows, :], NT).astype(BF)
+        c.rt[:, 0:384] = turned
+        ri = tile(i)
+
+        def block(k, _):
+            ki = tile(k)
+            c.a[ri, ki] = c.a[ri, ki] + dot(c.rt[:, 0:384], c.r[k, rows, :], NN)
+            return 0
+
+        lax.fori_loop(0, i + 1, block, 0)
+        return 0
+
+    lax.fori_loop(0, hi, strip, 0)
+
+
+def diagonal(c, p):
     c0, c1 = span(p * 256, 128), span(p * 256 + 128, 128)
-    event(2 * p)
-    chol128(lambda g: c.a[span(p * 256 + 8 * g, 8, 8), c0], c.u, c.i0)
-    c.a[c0, c0] = c.u[...].T
+    chol128(lambda g: c.a[span(p * 256 + 8 * g, 8, 8), c0], c.u0, c.i0)
     below = dot3(c.a[c1, c0], c.i0[...], NT)
+    c.a[c1, c1] = c.a[c1, c1] - dot3(below, below, NT)
+    chol128(lambda g: c.a[span(p * 256 + 128 + 8 * g, 8, 8), c1], c.u1, c.i1)
     c.a[c1, c0] = below
-    c.a[c1, c1] = c.a[c1, c1] - dot3(below, below, NT)
-    event(2 * p + 1)
-    chol128(lambda g: c.a[span(p * 256 + 128 + 8 * g, 8, 8), c1], c.u, c.i1)
-    c.a[c1, c1] = c.u[...].T
+    c.a[c0, c0] = c.u0[...].T
+    c.a[c1, c1] = c.u1[...].T
     corner = -dot3(c.i1[...], dot3(below, c.i0[...], NN), NN)
     zero = jnp.zeros((128, 128), F32)
     for rs, cs, v in ((0, 0, c.i0[...]), (0, 128, zero), (128, 0, corner), (128, 128, c.i1[...])):
         high, low = split(v)
         for at, part in ((0, high), (256, high), (512, low)):
             c.inv[p, rs : rs + 128, at + cs : at + cs + 128] = part
+
+
+def solved(c, v, q, rows, cols):
+    high, low = split(v)
+    x = dot(jnp.concatenate([high, low, high], axis=1), c.inv[q], NT)
+    c.a[rows, cols] = x
+    high, low = split(x)
+    c.lh[rows, cols] = high
+    c.ll[rows, cols] = low
+
+
+def lower_left(c):
+    for q in range(4):
+        cols = slice(256 * q, 256 * q + 256)
+        done = slice(0, 256 * q)
+
+        def half(i, _, q=q, cols=cols, done=done):
+            rows = span(1024 + 512 * i, 512)
+            v = c.a[rows, cols]
+            if q:
+                high, low = c.lh[rows, done], c.ll[rows, done]
+                other, other_low = c.lh[cols, done], c.ll[cols, done]
+                v = v - dot(
+                    jnp.concatenate([high, low, high], axis=1),
+                    jnp.concatenate([other, other, other_low], axis=1), NT)
+            solved(c, v, q, rows, cols)
+            return 0
+
+        lax.fori_loop(0, 2, half, 0)
+
+    def rest(t, _):
+        ti = tile(t)
+
+        def block(k, _):
+            ki = tile(k)
+            high, low = c.lh[ti, 0:1024], c.ll[ti, 0:1024]
+            other, other_low = c.lh[ki, 0:1024], c.ll[ki, 0:1024]
+            c.a[ti, ki] = c.a[ti, ki] - dot(
+                jnp.concatenate([high, low, high], axis=1),
+                jnp.concatenate([other, other, other_low], axis=1), NT)
+            return 0
+
+        lax.fori_loop(4, t + 1, block, 0)
+        return 0
+
+    lax.fori_loop(4, 8, rest, 0)
 
 
 def solve(c, p, lo, hi):
@@ -177,20 +297,21 @@
 
 
 def factor_scratch(n, rows):
+    square = pltpu.VMEM((128, 128), F32)
     return dict(
         a=pltpu.VMEM((n, n), F32), rt=pltpu.VMEM((256, rows), BF),
         lh=pltpu.VMEM((n, n), BF), ll=pltpu.VMEM((n, n), BF),
-        u=pltpu.VMEM((128, 128), F32), i0=pltpu.VMEM((128, 128), F32), i1=pltpu.VMEM((128, 128), F32),
+        u0=square, u1=square, i0=square, i1=square,
         inv=pltpu.VMEM((n // 256, 256, 768), BF),
     )
 
 
 def factor_steps(c, event, second):
-    make_normal(c, 0, 4)
-
     def panel(p, _):
         hi = 4 + 4 * (p // 4)
-        diagonal(c, p, event)
+        event(2 * p)
+        diagonal(c, p)
+        event(2 * p + 1)
         solve(c, p, p + 1, hi)
         update(c, p, p + 1, hi)
 
@@ -198,13 +319,7 @@
         def _():
             second()
             make_normal(c, 4, 8)
-
-            def again(q, _):
-                solve(c, q, 4, 8)
-                update(c, q, 4, 8)
-                return 0
-
-            lax.fori_loop(0, 4, again, 0)
+            lower_left(c)
 
         return 0
 
@@ -266,17 +381,17 @@
     return ((q % 2) * ((q + 1) // 2) + (1 - q % 2) * (8 - q // 2)) % 8
 
 
-NAMES = ("a", "rt", "lh", "ll", "u", "i0", "i1", "inv")
-
-
-def main_kernel(out_ref, lrow, lcol, frow, fcol, vrow, o_ref, r, ls, ss, rs, ys, yr, zs, zr, *scratch):
+NAMES = ("a", "rt", "lh", "ll", "u0", "u1", "i0", "i1", "inv")
+
+
+def main_kernel(out_ref, lrow, frow, vrow, o_ref, r, ls, ss, rs, ys, yr, zs, zr, *scratch):
     n = lax.axis_index("node")
     s = lax.axis_index("sector")
     z, w = n // 8, n % 8
     up, down = (s + 1) % 4, (s + 3) % 4
     there = (up, down)
     c = types.SimpleNamespace(
-        r=r, lrow=lrow, lcol=lcol, frow=frow, fcol=fcol, vrow=vrow, o=o_ref, **dict(zip(NAMES, scratch)))
+        r=r, lrow=lrow, frow=frow, vrow=vrow, o=o_ref, **dict(zip(NAMES, scratch)))
 
     def send(h, q, i):
         t = ((z + 8 - sequence(q)) % 8) * 8 + (w + 8 - i) % 8
@@ -314,12 +429,12 @@
         arriving(h, q, d).wait_recv()
         relay(h, q, d).start()
 
-    def finish(h):
+    def finish():
         def one(q, _):
-            arriving(h, 2 * q, 1).wait_recv()
-            arriving(h, 2 * q + 1, 0).wait_recv()
-            relayed(h, 2 * q).wait_recv()
-            relayed(h, 2 * q + 1).wait_recv()
+            arriving(1, 2 * q, 1).wait_recv()
+            arriving(1, 2 * q + 1, 0).wait_recv()
+            relayed(1, 2 * q).wait_recv()
+            relayed(1, 2 * q + 1).wait_recv()
             return 0
 
         lax.fori_loop(0, 4, one, 0)
@@ -345,6 +460,18 @@
         lax.fori_loop(1, 8, near, 0)
         lax.fori_loop(1, 8, far, 0)
 
+    start_normal(c, 4)
+
+    def gather(h, q, d):
+        arriving(h, q, 1 - d).wait_recv()
+        relayed(h, q).wait_recv()
+
+    def add(e):
+        for b in range(2):
+            q = 2 * e + b
+            gather(0, q, b)
+            add_rows(c, ((z + sequence(q)) % 8) * 384, 4)
+
     landed(0, 0, 7)
     mine[0].wait()
     forward(0, 0)
@@ -356,12 +483,22 @@
             landed(0, 2 * e + b, 8)
             forward(0, 2 * e + b)
             pass_on(0, 2 * e - 2 + b, b)
+
+        @pl.when(e > 1)
+        def _():
+            add(e - 2)
+
         return 0
 
     lax.fori_loop(1, 4, step, 0)
     pass_on(0, 6, 0)
     pass_on(0, 7, 1)
-    finish(0)
+
+    def rest(e, _):
+        add(e)
+        return 0
+
+    lax.fori_loop(2, 4, rest, 0)
 
     def event(e):
         @pl.when(e == 0)
@@ -383,7 +520,7 @@
             for b in range(2):
                 pass_on(1, 2 * e - 2 + b, b)
 
-    factor_steps(c, event, lambda: finish(1))
+    factor_steps(c, event, finish)
     write_band(c, s)
 
     for h in range(2):
@@ -410,12 +547,12 @@
     return pl.pallas_call(
         main_kernel,
         out_shape=jax.ShapeDtypeStruct((n // 4, n), F32),
-        in_specs=[pl.BlockSpec(memory_space=pl.ANY)] + [vmem] * 5,
+        in_specs=[pl.BlockSpec(memory_space=pl.ANY)] + [vmem] * 3,
         out_specs=vmem,
         scratch_shapes=[pltpu.VMEM((8, rows, 256), BF), dma((2,)), dma((2,)), dma((2, 8)), dma((2, 2)),
                         dma((2, 2, 8)), dma((2, 2)), dma((2, 8))] + [scratch[k] for k in NAMES],
         compiler_params=pltpu.CompilerParams(has_side_effects=True, vmem_limit_bytes=63 * 1024 * 1024),
-    )(outbox, labels[None, :], labels[:, None], loading[None, :], loading[:, None], variance[None, :])
+    )(outbox, labels.astype(F32)[None, :], loading[None, :], variance[None, :])
 
 
 def sector_labels(sector_sizes, count):

time: 264 us -> 231 us (0.88)
  Pallas kernels: 253 us -> 222 us
  local copies, waits for them, and re-layouts: 10.2 us -> 6.74 us
    pallas_call x1, Pallas kernels: 248 us -> 217 us  [exchange_and_factor(): pl.pallas_call(main_kernel, out_shape=jax.ShapeDtypeStruct((n // 4, n), F...]
where the time goes in v4:
time: 231 us; the launch traced here: 230 us
  Pallas kernels  222 us (96%)
  local copies, waits for them, and re-layouts  6.74 us (3%)
    pallas_call x1, Pallas kernels, exchange_and_factor(): pl.pallas_call(main_kernel, out_shape=jax.ShapeDtypeStruct((n // 4, n), F...  217 us
    pallas_call x1, Pallas kernels, prepare(): pl.pallas_call(prep_kernel, out_shape=jax.ShapeDtypeStruct((2, 64, rows *...  5.14 us
    unnamed x1, local copies, waits for them, and re-layouts  4.7 us

profile of v4, /device:TPU:98, one launch (start us, length us, event | category | flops | bytes accessed | tf_op | source)
XLA Modules:
  0.0 229.9 jit_solution(5487328092393041818)
XLA Ops:
  0.0 1.3 sqrt_bitcast_fusion.scale_ref
  1.3 0.7 copy.9
  2.0 0.1 reduce-window.8
  2.1 0.1 reduce
  2.2 0.1 convert_reduce_fusion
  2.4 0.6 convert_element_type.17
  3.0 5.1 %shard_map.64.out_ref = bf16[2,64,48,256]{3,2,1,0:T(8,128)(2,1)} custom-call(s32[1]{0:T(128)} %bitcast.s_ref, s32[1,128]{1,0:T(1,128)} %bitcast.12, f32[12,128]{1,0:T(8,128)} %sqrt_bitcast_fusion.scale_ref, bf16[12,128,2048]{2,1,0:T(8,128)(2,1)} %bitcast.8, bf16[12,128,2048]{2,1,0:T(8,128)(2,1)} %bitcast.9), custom_call_target="tpu_custom_call" | custom-call | tf_op jit(solution)/shard_map/pallas_call | solution.py:363
  8.1 217.0 %shard_map.65 = f32[512,2048]{1,0:T(8,128)} custom-call(bf16[2,64,48,256]{3,2,1,0:T(8,128)(2,1)} %shard_map.64.out_ref, f32[1,2048]{1,0:T(1,128)} %bitcast.11, f32[1,2048]{1,0:T(1,128)} %frow.1, f32[1,2048]{1,0:T(1,128)} %vrow.1), custom_call_target="tpu_custom_call" | custom-call | tf_op jit(solution)/shard_map/pallas_call | solution.py:547
  225.2 4.7 %copy.11 = f32[1,512,2048]{2,1,0:T(8,128)} copy(f32[1,512,2048]{2,1,0:T(8,128)} %bitcast.10) | data formatting | bytes 8388608

commit v5 on v4

v5 whole, which is shorter than its diff:
```python
import functools
import types

import jax
import jax.numpy as jnp
from jax import lax
from jax.experimental import pallas as pl
from jax.experimental.pallas import tpu as pltpu
from jax.sharding import PartitionSpec as P

F32 = jnp.float32
BF = jnp.bfloat16


def sub(x, k):
    return jnp.broadcast_to(x[k : k + 1, :], (8, 128))


def lane(x, k):
    return jnp.broadcast_to(x[:, k : k + 1], (8, 128))


def eliminate(p, pi, near, g, row):
    c = [lane(p, 8 * g + m) for m in range(8)]
    cs = [[lane(a, 8 * g + m) for m in range(8)] for a, _ in near]
    near = [list(x) for x in near]
    pivots = jnp.ones((8, 128), F32)
    for k in range(0, 8, 2):
        a, b, d = sub(c[k], k), sub(c[k + 1], k), sub(c[k + 1], k + 1)
        det = a * d - b * b
        ia = 1.0 / a
        id1 = a * (1.0 / det)
        ratio = b * ia
        m0 = jnp.where(row > k, c[k] * ia, 0.0)
        m1 = jnp.where(row > k + 1, (c[k + 1] - c[k] * ratio) * id1, 0.0)
        p0, pi0 = sub(p, k), sub(pi, k)
        p1, pi1 = sub(p, k + 1) - ratio * p0, sub(pi, k + 1) - ratio * pi0
        es = {}
        for m in range(k + 2, 8):
            e0 = sub(c[m], k)
            es[m] = (e0, sub(c[m], k + 1) - ratio * e0)
            c[m] = c[m] - m0 * es[m][0] - m1 * es[m][1]
        p = p - m0 * p0 - m1 * p1
        pi = pi - m0 * pi0 - m1 * pi1
        for x, cr in zip(near, cs):
            n0 = cr[k] * ia
            n1 = (cr[k + 1] - cr[k] * ratio) * id1
            for m in range(k + 2, 8):
                cr[m] = cr[m] - n0 * es[m][0] - n1 * es[m][1]
            x[0] = x[0] - n0 * p0 - n1 * p1
            x[1] = x[1] - n0 * pi0 - n1 * pi1
        pivots = jnp.where(row == k, a, jnp.where(row == k + 1, det * ia, pivots))
    scale = lax.rsqrt(pivots)
    return p * scale, pi * scale, near


def chol128(load, u_ref, inv_ref):
    row = lax.broadcasted_iota(jnp.int32, (8, 128), 0)
    col = lax.broadcasted_iota(jnp.int32, (8, 128), 1)
    n = 4
    wa = [load(g) for g in range(16)]
    wi = [jnp.where(col == row + 8 * g, 1.0, 0.0).astype(F32) for g in range(16)]
    for start in range(0, 16, n):
        qs, qis = [], []
        for g in range(start, start + n):
            near = [(wa[x], wi[x]) for x in range(g + 1, start + n)]
            q, qi, near = eliminate(wa[g], wi[g], near, g, row)
            for x, (a, b) in zip(range(g + 1, start + n), near):
                wa[x], wi[x] = a, b
            q = jnp.where(col >= row + 8 * g, q, 0.0)
            u_ref[8 * g : 8 * g + 8, :] = q
            inv_ref[8 * g : 8 * g + 8, :] = qi
            qs.append(q)
            qis.append(qi)
        if start + n < 16:
            q = jnp.concatenate(qs, axis=0)
            full = jnp.concatenate([q, jnp.concatenate(qis, axis=0)], axis=1)
            qh = full.astype(BF)
            ql = (full - qh.astype(F32)).astype(BF)
            left = jnp.concatenate([qh[:, :128], ql[:, :128], qh[:, :128]], axis=0)
            right = jnp.concatenate([qh, qh, ql], axis=0)
            moved = lax.dot_general(left, right, (((0,), (0,)), ((), ())), preferred_element_type=F32)
            for x in range(start + n, 16):
                wa[x] = wa[x] - moved[8 * x : 8 * x + 8, :128]
                wi[x] = wi[x] - moved[8 * x : 8 * x + 8, 128:]


NT = (((1,), (1,)), ((), ()))
NN = (((1,), (0,)), ((), ()))


def dot(a, b, dims):
    return lax.dot_general(a, b, dims, preferred_element_type=F32)


def split(x):
    high = x.astype(BF)
    return high, (x - high.astype(F32)).astype(BF)


def dot3(a, b, dims):
    ah, al = split(a)
    bh, bl = split(b)
    return dot(ah, bh, dims) + (dot(al, bh, dims) + dot(ah, bl, dims))


def tile(i, size=256):
    return pl.ds(pl.multiple_of(i * size, size), size)


def span(start, size, m=128):
    return pl.ds(pl.multiple_of(start, m), size)


def column(row_ref, cols):
    return jnp.broadcast_to(row_ref[:, cols], (256, 256)).T


def make_normal(c, lo, hi):
    ir = lax.broadcasted_iota(jnp.int32, (256, 256), 0)
    ic = lax.broadcasted_iota(jnp.int32, (256, 256), 1)
    eye = jnp.where(ir == ic, 1.0, 0.0).astype(BF)
    depth = c.r.shape[1]

    def strip(i, _):
        for part in range(depth // 512):
            rows = slice(part * 512, (part + 1) * 512)
            c.rt[:, rows] = dot(eye, c.r[i, rows, :], NT).astype(BF)
        ri = tile(i)
        labels = column(c.lrow, ri)
        loading = column(c.frow, ri)

        def block(k, _):
            ki = tile(k)
            total = dot(c.rt[...], c.r[k], NN)
            total = total + jnp.where(labels == c.lrow[:, ki], loading * c.frow[:, ki], 0.0)
            total = total + jnp.where((ir == ic) & (i == k), c.vrow[:, ki], 0.0)
            c.a[ri, ki] = total
            return 0

        lax.fori_loop(0, i + 1, block, 0)
        return 0

    lax.fori_loop(lo, hi, strip, 0)


def diagonal(c, p):
    c0, c1 = span(p * 256, 128), span(p * 256 + 128, 128)
    chol128(lambda g: c.a[span(p * 256 + 8 * g, 8, 8), c0], c.u0, c.i0)
    below = dot3(c.a[c1, c0], c.i0[...], NT)
    c.a[c1, c1] = c.a[c1, c1] - dot3(below, below, NT)
    chol128(lambda g: c.a[span(p * 256 + 128 + 8 * g, 8, 8), c1], c.u1, c.i1)
    c.a[c1, c0] = below
    c.a[c0, c0] = c.u0[...].T
    c.a[c1, c1] = c.u1[...].T
    corner = -dot3(c.i1[...], dot3(below, c.i0[...], NN), NN)
    zero = jnp.zeros((128, 128), F32)
    for rs, cs, v in ((0, 0, c.i0[...]), (0, 128, zero), (128, 0, corner), (128, 128, c.i1[...])):
        high, low = split(v)
        for at, part in ((0, high), (256, high), (512, low)):
            c.inv[p, rs : rs + 128, at + cs : at + cs + 128] = part


def finish_row(c, t):
    ti = tile(t)

    def panel(q, _):
        qi = tile(q)
        high, low = split(c.a[ti, qi])
        x = dot(jnp.concatenate([high, low, high], axis=1), c.inv[q], NT)
        c.a[ti, qi] = x
        high, low = split(x)
        c.lh[ti, qi] = high
        c.ll[ti, qi] = low

        def block(k, _):
            ki = tile(k)
            left, left_low = c.lh[ti, qi], c.ll[ti, qi]
            other, other_low = c.lh[ki, qi], c.ll[ki, qi]
            c.a[ti, ki] = c.a[ti, ki] - dot(
                jnp.concatenate([left, left_low, left], axis=1),
                jnp.concatenate([other, other, other_low], axis=1), NT)
            return 0

        lax.fori_loop(q + 1, t + 1, block, 0)
        return 0

    lax.fori_loop(0, t, panel, 0)


def write_band(c, s):
    n = c.a.shape[1]

    def rows(b, _):
        r0 = s * 512 + b * 64
        rr = lax.broadcasted_iota(jnp.int32, (64, n), 0) + r0
        cc = lax.broadcasted_iota(jnp.int32, (64, n), 1)
        c.o[tile(b, 64), :] = jnp.where(cc <= rr, c.a[span(r0, 64, 64), :], 0.0)
        return 0

    lax.fori_loop(0, 8, rows, 0)


def factor_scratch(n, rows):
    square = pltpu.VMEM((128, 128), F32)
    return dict(
        a=pltpu.VMEM((n, n), F32), rt=pltpu.VMEM((256, rows), BF),
        lh=pltpu.VMEM((n, n), BF), ll=pltpu.VMEM((n, n), BF),
        u0=square, u1=square, i0=square, i1=square,
        inv=pltpu.VMEM((n // 256, 256, 768), BF),
    )


def factor_steps(c, arrived, forward, pass_on):
    def row(t, _):
        arrived(t)
        make_normal(c, t, t + 1)
        forward(t + 2)
        finish_row(c, t)
        pass_on(t + 1)
        diagonal(c, t)
        return 0

    lax.fori_loop(0, 8, row, 0)


MESH = pl.DeviceIdType.MESH


def prep_kernel(at_ref, targets_ref, scale_ref, x_ref, o_ref, picks, scale):
    strip = pl.program_id(0)
    rows, children, width = x_ref.shape

    @pl.when(strip == 0)
    def _():
        targets = targets_ref[...]
        across = jnp.broadcast_to(targets.astype(F32), (children, children))
        first = lax.broadcasted_iota(jnp.int32, (children, children), 0)
        second = lax.broadcasted_iota(jnp.int32, (children, children), 1)
        earlier = (across.T == across) & (first < second)
        position = jnp.sum(jnp.where(earlier, 1.0, 0.0), axis=0, keepdims=True).astype(jnp.int32)
        slot = targets * 4 + position
        scale[...] = jnp.concatenate([scale_ref[...], jnp.zeros((16 - rows, children), F32)], axis=0).T
        height = picks.shape[0]
        out_row = lax.broadcasted_iota(jnp.int32, (height, children), 0)
        row_slot = (out_row // 16) * 4 + out_row % 4
        hit = row_slot == jnp.broadcast_to(slot, (height, children))
        lane_of = (out_row // 4) % 4
        for k in range(4):
            picks[:, k * children : (k + 1) * children] = jnp.where(hit & (lane_of == k), 1.0, 0.0).astype(BF)

    for quad in range(rows // 4):
        scaled = []
        for k in range(4):
            r = quad * 4 + k
            scaled.append((scale[:, r : r + 1] * x_ref[r].astype(F32)).astype(BF))
        scaled = jnp.concatenate(scaled, axis=0)
        for b in range(2):
            plane = lax.rem(at_ref[1] + 8 - (lax.rem(at_ref[0] + strip, 4) + 4 * b), 8)
            moved = dot(picks[span(plane * 128, 128), :], scaled, NN).astype(BF)
            o_ref[8 * b : 8 * b + 8, quad * 16 : (quad + 1) * 16, :] = moved.reshape(8, 16, width)


def prepare(at, targets, scale, planes):
    rows, children, assets = planes.shape
    width = 256
    return pl.pallas_call(
        prep_kernel,
        out_shape=jax.ShapeDtypeStruct((128, rows * 4, width), BF),
        grid_spec=pltpu.PrefetchScalarGridSpec(
            num_scalar_prefetch=1,
            grid=(assets // width,),
            in_specs=[
                pl.BlockSpec((1, children), lambda i, s: (0, 0)),
                pl.BlockSpec((rows, children), lambda i, s: (0, 0)),
                pl.BlockSpec((rows, children, width), lambda i, s: (0, 0, i)),
            ],
            out_specs=pl.BlockSpec((16, rows * 4, width), lambda i, s: (i, 0, 0)),
            scratch_shapes=[pltpu.VMEM((1024, 4 * children), BF), pltpu.VMEM((children, 16), F32)],
        ),
    )(at, targets, scale, planes)


NAMES = ("a", "rt", "lh", "ll", "u0", "u1", "i0", "i1", "inv")


def main_kernel(out_ref, lrow, frow, vrow, o_ref, r, ls, ss, rs, ys, yr, zs, zr, *scratch):
    n = lax.axis_index("node")
    s = lax.axis_index("sector")
    z, w = n // 8, n % 8
    there = ((s + 1) % 4, (s + 3) % 4)
    c = types.SimpleNamespace(
        r=r, lrow=lrow, frow=frow, vrow=vrow, o=o_ref, **dict(zip(NAMES, scratch)))

    def distance(t, b, sector):
        return (sector + t) % 4 + 4 * b

    def send(h, t, b, i):
        j = distance(t, b, s)
        other = (w + i) % 8
        pltpu.make_async_remote_copy(
            out_ref.at[(2 * t + b) * 8 + other], r.at[t, tile(n, 48)], ss.at[h], rs.at[t, b],
            device_id=(((z + 8 - j) % 8) * 8 + other, s), device_id_type=MESH).start()

    def landed(t, b, count):
        rows = r.at[t, span(((z + distance(t, b, s)) % 8) * 384, 48 * count, 48)]
        pltpu.make_async_remote_copy(
            rows, rows, ss.at[0], rs.at[t, b], device_id=(n, there[0]), device_id_type=MESH).wait_recv()

    def group(t, b, sector, d, sent, got):
        rows = r.at[t, tile((z + distance(t, b, sector)) % 8, 384)]
        return pltpu.make_async_remote_copy(
            rows, rows, sent, got, device_id=(n, there[d]), device_id_type=MESH)

    def own(t, b, d):
        return group(t, b, s, d, ys.at[d], yr.at[t, d, b])

    def arriving(t, b, d):
        return group(t, b, there[1 - d], d, ys.at[d], yr.at[t, d, b])

    def relay(t, b):
        return group(t, b, there[1 - b], b, zs.at[b], zr.at[t, b])

    def relayed(t, b):
        return group(t, b, (s + 2) % 4, b, zs.at[b], zr.at[t, b])

    def kept(h):
        t = (4 - s) % 4 + 4 * h
        return pltpu.make_async_copy(out_ref.at[16 * t + w], r.at[t, tile(n, 48)], ls.at[h])

    def forward(t):
        @pl.when(t < 8)
        def _():
            @pl.when(distance(t, 0, s) == 0)
            def _():
                landed(t, 0, 7)
                kept(t // 4).wait()

            @pl.when(distance(t, 0, s) > 0)
            def _():
                landed(t, 0, 8)

            own(t, 0, 0).start()
            own(t, 0, 1).start()
            landed(t, 1, 8)
            own(t, 1, 0).start()
            own(t, 1, 1).start()

    def pass_on(t):
        @pl.when(t < 8)
        def _():
            for b in range(2):
                arriving(t, b, b).wait_recv()
                relay(t, b).start()

    def arrived(t):
        for b in range(2):
            arriving(t, b, 1 - b).wait_recv()
            relayed(t, b).wait_recv()

    for h in range(2):
        kept(h).start()

        def strip(t, _, h=h):
            for b in range(2):
                def one(i, _, b=b):
                    send(h, t, b, i)
                    return 0

                lax.fori_loop((8 - distance(t, b, s)) // 8, 8, one, 0)
            return 0

        lax.fori_loop(4 * h, 4 * h + 4, strip, 0)

    forward(jnp.int32(0))
    forward(jnp.int32(1))
    pass_on(jnp.int32(0))
    factor_steps(c, arrived, forward, pass_on)
    write_band(c, s)

    for h in range(2):
        blocks = out_ref.at[pl.ds(0, 63)]
        pltpu.make_async_remote_copy(
            blocks, blocks, ss.at[h], rs.at[0, 0], device_id=(n, there[0]), device_id_type=MESH
        ).wait_send()
    for d in range(2):
        pair = r.at[pl.ds(0, 2)]
        pltpu.make_async_remote_copy(
            pair, pair, ys.at[d], yr.at[0, d, 0], device_id=(n, there[0]), device_id_type=MESH
        ).wait_send()
        pltpu.make_async_remote_copy(
            r.at[0], r.at[0], zs.at[d], zr.at[0, 0], device_id=(n, there[0]), device_id_type=MESH
        ).wait_send()


def exchange_and_factor(outbox, labels, loading, variance):
    dma = pltpu.SemaphoreType.DMA
    n = labels.shape[0]
    rows = outbox.shape[1] * 64
    vmem = pl.BlockSpec(memory_space=pltpu.VMEM)
    scratch = factor_scratch(n, rows)
    return pl.pallas_call(
        main_kernel,
        out_shape=jax.ShapeDtypeStruct((n // 4, n), F32),
        in_specs=[pl.BlockSpec(memory_space=pl.ANY)] + [vmem] * 3,
        out_specs=vmem,
        scratch_shapes=[pltpu.VMEM((8, rows, 256), BF), dma((2,)), dma((2,)), dma((8, 2)), dma((2,)),
                        dma((8, 2, 2)), dma((2,)), dma((8, 2))] + [scratch[k] for k in NAMES],
        compiler_params=pltpu.CompilerParams(has_side_effects=True, vmem_limit_bytes=63 * 1024 * 1024),
    )(outbox, labels.astype(F32)[None, :], loading[None, :], variance[None, :])


def sector_labels(sector_sizes, count):
    sector_ends = jnp.cumsum(sector_sizes)
    asset_index = jnp.arange(count, dtype=jnp.int32)
    return jnp.sum((asset_index[:, None] >= sector_ends[None, :]).astype(jnp.int32), axis=1)


def on_device(returns, barrier_scale, parent_ids, loadings, own_variance, sector_sizes):
    child_count, row_count, asset_count = returns.shape
    at = jnp.stack([lax.axis_index("sector"), lax.axis_index("node") // 8]).astype(jnp.int32)
    outbox = prepare(
        at,
        parent_ids.reshape(1, child_count),
        jnp.sqrt(barrier_scale).T,
        returns.transpose(1, 0, 2),
    )
    labels = sector_labels(sector_sizes, asset_count)
    out = exchange_and_factor(outbox, labels, loadings[0], own_variance[0])
    return out[None]


def solution(mesh):
    in_specs = (
        P("node", None, None),
        P("node", None),
        P("node", None),
        P("node", None),
        P("node", None),
        P(),
    )
    return jax.shard_map(
        on_device, mesh=mesh, in_specs=in_specs, out_specs=P("node", "sector", None), check_vma=False
    )
```

time: 231 us -> 230 us (level)
    pallas_call x1, Pallas kernels: 217 us -> 212 us  [exchange_and_factor(): pl.pallas_call(main_kernel, out_shape=jax.ShapeDtypeStruct((n // 4, n), F...]
    pallas_call x1, Pallas kernels: 5.14 us -> 9.76 us  [prepare(): pl.pallas_call(prep_kernel, out_shape=jax.ShapeDtypeStruct((128, rows * 4...]
where the time goes in v5:
time: 230 us
  Pallas kernels  222 us (97%)
  local copies, waits for them, and re-layouts  6.74 us (3%)
    pallas_call x1, Pallas kernels, exchange_and_factor(): pl.pallas_call(main_kernel, out_shape=jax.ShapeDtypeStruct((n // 4, n), F...  212 us
    pallas_call x1, Pallas kernels, prepare(): pl.pallas_call(prep_kernel, out_shape=jax.ShapeDtypeStruct((128, rows * 4...  9.76 us
    unnamed x1, local copies, waits for them, and re-layouts  4.7 us

profile of v5, /device:TPU:98, one launch (start us, length us, event | category | flops | bytes accessed | tf_op | source)
XLA Modules:
  0.0 229.9 jit_solution(4319215031346013014)
XLA Ops:
  0.0 0.6 pad_add_fusion.at_ref
  0.6 1.3 sqrt_bitcast_fusion.scale_ref
  1.9 0.7 copy.9
  2.6 0.1 reduce-window.8
  2.7 0.1 reduce
  2.8 0.1 convert_reduce_fusion
  3.0 0.6 convert_element_type.17
  3.6 9.8 %shard_map.64.out_ref = bf16[128,48,256]{2,1,0:T(8,128)(2,1)} custom-call(s32[2]{0:T(128)} %pad_add_fusion.at_ref, s32[1,128]{1,0:T(1,128)} %bitcast.13, f32[12,128]{1,0:T(8,128)} %sqrt_bitcast_fusion.scale_ref, bf16[12,128,2048]{2,1,0:T(8,128)(2,1)} %bitcast.10), custom_call_target="tpu_custom_call" | custom-call | tf_op jit(solution)/shard_map/pallas_call | solution.py:267
  13.3 211.9 %shard_map.65 = f32[512,2048]{1,0:T(8,128)} custom-call(bf16[128,48,256]{2,1,0:T(8,128)(2,1)} %shard_map.64.out_ref, f32[1,2048]{1,0:T(1,128)} %bitcast.11, f32[1,2048]{1,0:T(1,128)} %frow.1, f32[1,2048]{1,0:T(1,128)} %vrow.1), custom_call_target="tpu_custom_call" | custom-call | tf_op jit(solution)/shard_map/pallas_call | solution.py:402
  225.2 4.7 %copy.11 = f32[1,512,2048]{2,1,0:T(8,128)} copy(f32[1,512,2048]{2,1,0:T(8,128)} %bitcast.9) | data formatting | bytes 8388608

commit v6 on v5

--- a/solution.py
+++ b/solution.py
@@ -144,9 +144,10 @@
     lax.fori_loop(lo, hi, strip, 0)
 
 
-def diagonal(c, p):
+def diagonal(c, p, between):
     c0, c1 = span(p * 256, 128), span(p * 256 + 128, 128)
     chol128(lambda g: c.a[span(p * 256 + 8 * g, 8, 8), c0], c.u0, c.i0)
+    between()
     below = dot3(c.a[c1, c0], c.i0[...], NT)
     c.a[c1, c1] = c.a[c1, c1] - dot3(below, below, NT)
     chol128(lambda g: c.a[span(p * 256 + 128 + 8 * g, 8, 8), c1], c.u1, c.i1)
@@ -173,16 +174,25 @@
         c.lh[ti, qi] = high
         c.ll[ti, qi] = low
 
-        def block(k, _):
-            ki = tile(k)
+        def take_off(k, wide):
+            ki = span(k * 256, wide)
             left, left_low = c.lh[ti, qi], c.ll[ti, qi]
             other, other_low = c.lh[ki, qi], c.ll[ki, qi]
             c.a[ti, ki] = c.a[ti, ki] - dot(
                 jnp.concatenate([left, left_low, left], axis=1),
                 jnp.concatenate([other, other, other_low], axis=1), NT)
+
+        count = t - q
+
+        @pl.when(count % 2 == 1)
+        def _():
+            take_off(q + 1, 256)
+
+        def pair(e, _):
+            take_off(q + 1 + count % 2 + 2 * e, 512)
             return 0
 
-        lax.fori_loop(q + 1, t + 1, block, 0)
+        lax.fori_loop(0, count // 2, pair, 0)
         return 0
 
     lax.fori_loop(0, t, panel, 0)
@@ -214,11 +224,12 @@
 def factor_steps(c, arrived, forward, pass_on):
     def row(t, _):
         arrived(t)
+        forward(t + 2, 0)
         make_normal(c, t, t + 1)
-        forward(t + 2)
+        pass_on(t + 1, 1)
         finish_row(c, t)
-        pass_on(t + 1)
-        diagonal(c, t)
+        forward(t + 2, 1)
+        diagonal(c, t, lambda: pass_on(t + 2, 0))
         return 0
 
     lax.fori_loop(0, 8, row, 0)
@@ -328,30 +339,29 @@
         t = (4 - s) % 4 + 4 * h
         return pltpu.make_async_copy(out_ref.at[16 * t + w], r.at[t, tile(n, 48)], ls.at[h])
 
-    def forward(t):
+    def forward(t, b):
         @pl.when(t < 8)
         def _():
-            @pl.when(distance(t, 0, s) == 0)
-            def _():
-                landed(t, 0, 7)
-                kept(t // 4).wait()
-
-            @pl.when(distance(t, 0, s) > 0)
-            def _():
-                landed(t, 0, 8)
-
-            own(t, 0, 0).start()
-            own(t, 0, 1).start()
-            landed(t, 1, 8)
-            own(t, 1, 0).start()
-            own(t, 1, 1).start()
-
-    def pass_on(t):
+            if b:
+                landed(t, 1, 8)
+            else:
+                @pl.when(distance(t, 0, s) == 0)
+                def _():
+                    landed(t, 0, 7)
+                    kept(t // 4).wait()
+
+                @pl.when(distance(t, 0, s) > 0)
+                def _():
+                    landed(t, 0, 8)
+
+            own(t, b, 0).start()
+            own(t, b, 1).start()
+
+    def pass_on(t, b):
         @pl.when(t < 8)
         def _():
-            for b in range(2):
-                arriving(t, b, b).wait_recv()
-                relay(t, b).start()
+            arriving(t, b, b).wait_recv()
+            relay(t, b).start()
 
     def arrived(t):
         for b in range(2):
@@ -372,9 +382,14 @@
 
         lax.fori_loop(4 * h, 4 * h + 4, strip, 0)
 
-    forward(jnp.int32(0))
-    forward(jnp.int32(1))
-    pass_on(jnp.int32(0))
+    first, second = jnp.int32(0), jnp.int32(1)
+    forward(first, 0)
+    forward(first, 1)
+    pass_on(first, 0)
+    forward(second, 0)
+    pass_on(first, 1)
+    forward(second, 1)
+    pass_on(second, 0)
     factor_steps(c, arrived, forward, pass_on)
     write_band(c, s)
 

time: 230 us -> 210 us (0.913)
  the two profiles are of different devices: /device:TPU:98 before, /device:TPU:33 now
where the time goes in v6:
time: 210 us; the launch traced here: 209 us
  Pallas kernels  201 us (96%)
  local copies, waits for them, and re-layouts  6.74 us (3%)
    pallas_call x1, Pallas kernels, exchange_and_factor(): pl.pallas_call(main_kernel, out_shape=jax.ShapeDtypeStruct((n // 4, n), F...  191 us
    pallas_call x1, Pallas kernels, prepare(): pl.pallas_call(prep_kernel, out_shape=jax.ShapeDtypeStruct((128, rows * 4...  9.76 us
    unnamed x1, local copies, waits for them, and re-layouts  4.7 us

profile of v6, /device:TPU:33, one launch (start us, length us, event | category | flops | bytes accessed | tf_op | source)
XLA Modules:
  0.0 209.3 jit_solution(8441751197140150737)
XLA Ops:
  0.0 0.6 pad_add_fusion.at_ref
  0.6 1.3 sqrt_bitcast_fusion.scale_ref
  1.9 0.7 copy.9
  2.6 0.1 reduce-window.8
  2.7 0.1 reduce
  2.8 0.1 convert_reduce_fusion
  3.0 0.6 convert_element_type.17
  3.6 9.8 %shard_map.64.out_ref = bf16[128,48,256]{2,1,0:T(8,128)(2,1)} custom-call(s32[2]{0:T(128)} %pad_add_fusion.at_ref, s32[1,128]{1,0:T(1,128)} %bitcast.13, f32[12,128]{1,0:T(8,128)} %sqrt_bitcast_fusion.scale_ref, bf16[12,128,2048]{2,1,0:T(8,128)(2,1)} %bitcast.10), custom_call_target="tpu_custom_call" | custom-call | tf_op jit(solution)/shard_map/pallas_call | solution.py:278
  13.3 191.3 %shard_map.65 = f32[512,2048]{1,0:T(8,128)} custom-call(bf16[128,48,256]{2,1,0:T(8,128)(2,1)} %shard_map.64.out_ref, f32[1,2048]{1,0:T(1,128)} %bitcast.11, f32[1,2048]{1,0:T(1,128)} %frow.1, f32[1,2048]{1,0:T(1,128)} %vrow.1), custom_call_target="tpu_custom_call" | custom-call | tf_op jit(solution)/shard_map/pallas_call | solution.py:417
  204.6 4.7 %copy.11 = f32[1,512,2048]{2,1,0:T(8,128)} copy(f32[1,512,2048]{2,1,0:T(8,128)} %bitcast.9) | data formatting | bytes 8388608

commit v7 on v6

--- a/solution.py
+++ b/solution.py
@@ -144,10 +144,13 @@
     lax.fori_loop(lo, hi, strip, 0)
 
 
-def diagonal(c, p, between):
+def diagonal_first(c, p):
+    c0 = span(p * 256, 128)
+    chol128(lambda g: c.a[span(p * 256 + 8 * g, 8, 8), c0], c.u0, c.i0)
+
+
+def diagonal_second(c, p):
     c0, c1 = span(p * 256, 128), span(p * 256 + 128, 128)
-    chol128(lambda g: c.a[span(p * 256 + 8 * g, 8, 8), c0], c.u0, c.i0)
-    between()
     below = dot3(c.a[c1, c0], c.i0[...], NT)
     c.a[c1, c1] = c.a[c1, c1] - dot3(below, below, NT)
     chol128(lambda g: c.a[span(p * 256 + 128 + 8 * g, 8, 8), c1], c.u1, c.i1)
@@ -221,15 +224,22 @@
     )
 
 
-def factor_steps(c, arrived, forward, pass_on):
+def factor_steps(c, needs, arrived, forward, pass_on):
     def row(t, _):
+        def if_needed(step):
+            @pl.when(needs(t))
+            def _():
+                step()
+
         arrived(t)
         forward(t + 2, 0)
-        make_normal(c, t, t + 1)
+        if_needed(lambda: make_normal(c, t, t + 1))
         pass_on(t + 1, 1)
-        finish_row(c, t)
+        if_needed(lambda: finish_row(c, t))
         forward(t + 2, 1)
-        diagonal(c, t, lambda: pass_on(t + 2, 0))
+        if_needed(lambda: diagonal_first(c, t))
+        pass_on(t + 2, 0)
+        if_needed(lambda: diagonal_second(c, t))
         return 0
 
     lax.fori_loop(0, 8, row, 0)
@@ -266,10 +276,12 @@
             r = quad * 4 + k
             scaled.append((scale[:, r : r + 1] * x_ref[r].astype(F32)).astype(BF))
         scaled = jnp.concatenate(scaled, axis=0)
+        chosen = []
         for b in range(2):
             plane = lax.rem(at_ref[1] + 8 - (lax.rem(at_ref[0] + strip, 4) + 4 * b), 8)
-            moved = dot(picks[span(plane * 128, 128), :], scaled, NN).astype(BF)
-            o_ref[8 * b : 8 * b + 8, quad * 16 : (quad + 1) * 16, :] = moved.reshape(8, 16, width)
+            chosen.append(picks[span(plane * 128, 128), :])
+        moved = dot(jnp.concatenate(chosen, axis=0), scaled, NN).astype(BF)
+        o_ref[:, quad * 16 : (quad + 1) * 16, :] = moved.reshape(16, 16, width)
 
 
 def prepare(at, targets, scale, planes):
@@ -324,20 +336,28 @@
             rows, rows, sent, got, device_id=(n, there[d]), device_id_type=MESH)
 
     def own(t, b, d):
-        return group(t, b, s, d, ys.at[d], yr.at[t, d, b])
+        return group(t, b, s, d, ys.at[t, d, b], yr.at[t, d, b])
 
     def arriving(t, b, d):
-        return group(t, b, there[1 - d], d, ys.at[d], yr.at[t, d, b])
+        return group(t, b, there[1 - d], d, ys.at[t, d, b], yr.at[t, d, b])
 
     def relay(t, b):
-        return group(t, b, there[1 - b], b, zs.at[b], zr.at[t, b])
+        return group(t, b, there[1 - b], b, zs.at[t, b], zr.at[t, b])
 
     def relayed(t, b):
-        return group(t, b, (s + 2) % 4, b, zs.at[b], zr.at[t, b])
+        return group(t, b, (s + 2) % 4, b, zs.at[t, b], zr.at[t, b])
 
     def kept(h):
         t = (4 - s) % 4 + 4 * h
         return pltpu.make_async_copy(out_ref.at[16 * t + w], r.at[t, tile(n, 48)], ls.at[h])
+
+    def needs(t, sector):
+        return 2 * sector + 1 >= t
+
+    def wanted(t, b, d):
+        if b == d:
+            return needs(t, there[d]) | needs(t, (s + 2) % 4)
+        return needs(t, there[d])
 
     def forward(t, b):
         @pl.when(t < 8)
@@ -354,19 +374,28 @@
                 def _():
                     landed(t, 0, 8)
 
-            own(t, b, 0).start()
-            own(t, b, 1).start()
+            for d in range(2):
+                @pl.when(wanted(t, b, d))
+                def _(d=d):
+                    own(t, b, d).start()
 
     def pass_on(t, b):
         @pl.when(t < 8)
         def _():
-            arriving(t, b, b).wait_recv()
-            relay(t, b).start()
+            @pl.when(needs(t, s) | needs(t, there[b]))
+            def _():
+                arriving(t, b, b).wait_recv()
+
+            @pl.when(needs(t, there[b]))
+            def _():
+                relay(t, b).start()
 
     def arrived(t):
-        for b in range(2):
-            arriving(t, b, 1 - b).wait_recv()
-            relayed(t, b).wait_recv()
+        @pl.when(needs(t, s))
+        def _():
+            for b in range(2):
+                arriving(t, b, 1 - b).wait_recv()
+                relayed(t, b).wait_recv()
 
     for h in range(2):
         kept(h).start()
@@ -390,7 +419,7 @@
     pass_on(first, 1)
     forward(second, 1)
     pass_on(second, 0)
-    factor_steps(c, arrived, forward, pass_on)
+    factor_steps(c, lambda t: needs(t, s), arrived, forward, pass_on)
     write_band(c, s)
 
     for h in range(2):
@@ -398,14 +427,19 @@
         pltpu.make_async_remote_copy(
             blocks, blocks, ss.at[h], rs.at[0, 0], device_id=(n, there[0]), device_id_type=MESH
         ).wait_send()
-    for d in range(2):
-        pair = r.at[pl.ds(0, 2)]
-        pltpu.make_async_remote_copy(
-            pair, pair, ys.at[d], yr.at[0, d, 0], device_id=(n, there[0]), device_id_type=MESH
-        ).wait_send()
-        pltpu.make_async_remote_copy(
-            r.at[0], r.at[0], zs.at[d], zr.at[0, 0], device_id=(n, there[0]), device_id_type=MESH
-        ).wait_send()
+    def sent(t, _):
+        for b in range(2):
+            for d in range(2):
+                @pl.when(wanted(t, b, d))
+                def _(b=b, d=d):
+                    own(t, b, d).wait_send()
+
+            @pl.when(needs(t, there[b]))
+            def _(b=b):
+                relay(t, b).wait_send()
+        return 0
+
+    lax.fori_loop(0, 8, sent, 0)
 
 
 def exchange_and_factor(outbox, labels, loading, variance):
@@ -419,8 +453,8 @@
         out_shape=jax.ShapeDtypeStruct((n // 4, n), F32),
         in_specs=[pl.BlockSpec(memory_space=pl.ANY)] + [vmem] * 3,
         out_specs=vmem,
-        scratch_shapes=[pltpu.VMEM((8, rows, 256), BF), dma((2,)), dma((2,)), dma((8, 2)), dma((2,)),
-                        dma((8, 2, 2)), dma((2,)), dma((8, 2))] + [scratch[k] for k in NAMES],
+        scratch_shapes=[pltpu.VMEM((8, rows, 256), BF), dma((2,)), dma((2,)), dma((8, 2)), dma((8, 2, 2)),
+                        dma((8, 2, 2)), dma((8, 2)), dma((8, 2))] + [scratch[k] for k in NAMES],
         compiler_params=pltpu.CompilerParams(has_side_effects=True, vmem_limit_bytes=63 * 1024 * 1024),
     )(outbox, labels.astype(F32)[None, :], loading[None, :], variance[None, :])
 

time: 210 us -> 205 us (0.976)
  the two profiles are of different devices: /device:TPU:33 before, /device:TPU:121 now
where the time goes in v7:
time: 205 us
  Pallas kernels  197 us (96%)
  local copies, waits for them, and re-layouts  6.74 us (3%)
    pallas_call x1, Pallas kernels, exchange_and_factor(): pl.pallas_call(main_kernel, out_shape=jax.ShapeDtypeStruct((n // 4, n), F...  186 us
    pallas_call x1, Pallas kernels, prepare(): pl.pallas_call(prep_kernel, out_shape=jax.ShapeDtypeStruct((128, rows * 4...  10.4 us
    unnamed x1, local copies, waits for them, and re-layouts  4.7 us

profile of v7, /device:TPU:121, one launch (start us, length us, event | category | flops | bytes accessed | tf_op | source)
XLA Modules:
  0.0 204.9 jit_solution(8669197354224189528)
XLA Ops:
  0.0 0.6 pad_add_fusion.at_ref
  0.6 1.3 sqrt_bitcast_fusion.scale_ref
  1.9 0.7 copy.9
  2.6 0.1 reduce-window.8
  2.7 0.1 reduce
  2.8 0.1 convert_reduce_fusion
  3.0 0.6 convert_element_type.17
  3.6 10.4 %shard_map.64.out_ref = bf16[128,48,256]{2,1,0:T(8,128)(2,1)} custom-call(s32[2]{0:T(128)} %pad_add_fusion.at_ref, s32[1,128]{1,0:T(1,128)} %bitcast.13, f32[12,128]{1,0:T(8,128)} %sqrt_bitcast_fusion.scale_ref, bf16[12,128,2048]{2,1,0:T(8,128)(2,1)} %bitcast.10), custom_call_target="tpu_custom_call" | custom-call | tf_op jit(solution)/shard_map/pallas_call | solution.py:290
  14.0 186.2 %shard_map.65 = f32[512,2048]{1,0:T(8,128)} custom-call(bf16[128,48,256]{2,1,0:T(8,128)(2,1)} %shard_map.64.out_ref, f32[1,2048]{1,0:T(1,128)} %bitcast.11, f32[1,2048]{1,0:T(1,128)} %frow.1, f32[1,2048]{1,0:T(1,128)} %vrow.1), custom_call_target="tpu_custom_call" | custom-call | tf_op jit(solution)/shard_map/pallas_call | solution.py:451
  200.2 4.7 %copy.11 = f32[1,512,2048]{2,1,0:T(8,128)} copy(f32[1,512,2048]{2,1,0:T(8,128)} %bitcast.9) | data formatting | bytes 8388608

commit v8 on v7

--- a/solution.py
+++ b/solution.py
@@ -191,11 +191,14 @@
         def _():
             take_off(q + 1, 256)
 
-        def pair(e, _):
-            take_off(q + 1 + count % 2 + 2 * e, 512)
-            return 0
-
-        lax.fori_loop(0, count // 2, pair, 0)
+        @pl.when((count // 2) % 2 == 1)
+        def _():
+            take_off(q + 1 + count % 2, 512)
+
+        @pl.when(count > 3)
+        def _():
+            take_off(t - 3, 1024)
+
         return 0
 
     lax.fori_loop(0, t, panel, 0)
@@ -276,12 +279,10 @@
             r = quad * 4 + k
             scaled.append((scale[:, r : r + 1] * x_ref[r].astype(F32)).astype(BF))
         scaled = jnp.concatenate(scaled, axis=0)
-        chosen = []
         for b in range(2):
             plane = lax.rem(at_ref[1] + 8 - (lax.rem(at_ref[0] + strip, 4) + 4 * b), 8)
-            chosen.append(picks[span(plane * 128, 128), :])
-        moved = dot(jnp.concatenate(chosen, axis=0), scaled, NN).astype(BF)
-        o_ref[:, quad * 16 : (quad + 1) * 16, :] = moved.reshape(16, 16, width)
+            moved = dot(picks[span(plane * 128, 128), :], scaled, NN).astype(BF)
+            o_ref[8 * b : 8 * b + 8, quad * 16 : (quad + 1) * 16, :] = moved.reshape(8, 16, width)
 
 
 def prepare(at, targets, scale, planes):

time: 205 us -> 203 us (level)
  Pallas kernels: 197 us -> 194 us
where the time goes in v8:
time: 203 us
  Pallas kernels  194 us (96%)
  local copies, waits for them, and re-layouts  6.74 us (3%)
    pallas_call x1, Pallas kernels, exchange_and_factor(): pl.pallas_call(main_kernel, out_shape=jax.ShapeDtypeStruct((n // 4, n), F...  184 us
    pallas_call x1, Pallas kernels, prepare(): pl.pallas_call(prep_kernel, out_shape=jax.ShapeDtypeStruct((128, rows * 4...  9.76 us
    unnamed x1, local copies, waits for them, and re-layouts  4.7 us

profile of v8, /device:TPU:121, one launch (start us, length us, event | category | flops | bytes accessed | tf_op | source)
XLA Modules:
  0.0 202.5 jit_solution(7419032575484070241)
XLA Ops:
  0.0 0.6 pad_add_fusion.at_ref
  0.6 1.3 sqrt_bitcast_fusion.scale_ref
  1.9 0.7 copy.9
  2.6 0.1 reduce-window.8
  2.7 0.1 reduce
  2.8 0.1 convert_reduce_fusion
  3.0 0.6 convert_element_type.17
  3.6 9.8 %shard_map.64.out_ref = bf16[128,48,256]{2,1,0:T(8,128)(2,1)} custom-call(s32[2]{0:T(128)} %pad_add_fusion.at_ref, s32[1,128]{1,0:T(1,128)} %bitcast.13, f32[12,128]{1,0:T(8,128)} %sqrt_bitcast_fusion.scale_ref, bf16[12,128,2048]{2,1,0:T(8,128)(2,1)} %bitcast.10), custom_call_target="tpu_custom_call" | custom-call | tf_op jit(solution)/shard_map/pallas_call | solution.py:291
  13.3 184.5 %shard_map.65 = f32[512,2048]{1,0:T(8,128)} custom-call(bf16[128,48,256]{2,1,0:T(8,128)(2,1)} %shard_map.64.out_ref, f32[1,2048]{1,0:T(1,128)} %bitcast.11, f32[1,2048]{1,0:T(1,128)} %frow.1, f32[1,2048]{1,0:T(1,128)} %vrow.1), custom_call_target="tpu_custom_call" | custom-call | tf_op jit(solution)/shard_map/pallas_call | solution.py:452
  197.8 4.7 %copy.11 = f32[1,512,2048]{2,1,0:T(8,128)} copy(f32[1,512,2048]{2,1,0:T(8,128)} %bitcast.9) | data formatting | bytes 8388608
